TPU v7x, 32 devices: a whole 2x2x4 slice. The times are simulated.
32 devices in a mesh: group: 2 (over y), dp: 8 (over z, x), tensor: 2 (over core).
Axes of the slice: x: 2, y: 2, z: 4, core: 2. Of those that a mesh axis runs over, the one named last changes fastest.
Arguments:
- inputs: bfloat16 [12288, 1536], P(('group', 'dp')), may hold values from -6 to 6
- cotangent: bfloat16 [12288, 1536], P(('group', 'dp')), may hold values from -6 to 6
- lengths: int32 [16, 3], P(('group', 'dp')), may hold values from 1 to 576, 768 in all within a row
- attn_gain: bfloat16 [1536], P('dp'), may hold values from 0.25 to 1.75
- w_query: bfloat16 [1536, 1536], P('dp', 'tensor'), may hold values from -0.15625 to 0.15625
- b_query: bfloat16 [1536], P('tensor'), may hold values from -3 to 3
- w_key: bfloat16 [1536, 256], P('dp', 'tensor'), may hold values from -0.15625 to 0.15625
- b_key: bfloat16 [256], P('tensor'), may hold values from -3 to 3
- w_value: bfloat16 [1536, 256], P('dp', 'tensor'), may hold values from -0.15625 to 0.15625
- b_value: bfloat16 [256], P('tensor'), may hold values from -3 to 3
- w_out: bfloat16 [1536, 1536], P('dp', 'tensor'), may hold values from -1.25 to 1.25
- ffn_gain: bfloat16 [1536], P('dp'), may hold values from 0.25 to 1.75
- w_gate: bfloat16 [1536, 8960], P('dp', 'tensor'), may hold values from -0.15625 to 0.15625
- w_up: bfloat16 [1536, 8960], P('dp', 'tensor'), may hold values from -0.15625 to 0.15625
- w_down: bfloat16 [1536, 8960], P('dp', 'tensor'), may hold values from -0.0625 to 0.0625
Outputs:
- layer_out: bfloat16 [12288, 1536], P(('group', 'dp'))
- input_grad: bfloat16 [12288, 1536], P(('group', 'dp'))
- attn_gain_grad: float32 [1536], P('dp')
- w_query_grad: float32 [1536, 1536], P('dp', 'tensor')
- b_query_grad: float32 [1536], P('tensor')
- w_key_grad: float32 [1536, 256], P('dp', 'tensor')
- b_key_grad: float32 [256], P('tensor')
- w_value_grad: float32 [1536, 256], P('dp', 'tensor')
- b_value_grad: float32 [256], P('tensor')
- w_out_grad: float32 [1536, 1536], P('dp', 'tensor')
- ffn_gain_grad: float32 [1536], P('dp')
- w_gate_grad: float32 [1536, 8960], P('dp', 'tensor')
- w_up_grad: float32 [1536, 8960], P('dp', 'tensor')
- w_down_grad: float32 [1536, 8960], P('dp', 'tensor')
Inputs may be any that keep to these rules, and one draw needn't show every extreme that they name: In every stream the 3 lengths sum to 768, and the longest is exactly 576.
All inputs are finite; a program needn't handle non-finite values.
Results may differ from a plain program's by a relative error of at most 0.017.
Values may be sent and summed in bfloat16 or wider, within the bound.
No kernel may reach another device: no remote copies, remote signals or barrier semaphores. Data moves between devices by JAX's collectives and lax.ppermute only.
A program may use at most 384 MiB of HBM per device.

v0:
```python
import math

import jax
import jax.numpy as jnp
from jax import lax
from jax.experimental import pallas as pl
from jax.experimental.pallas import tpu as pltpu
from jax.sharding import PartitionSpec as P

HD = 128
SEQ = 768
NSEG = 3


EPSILON = 1e-06
THETA = 10000.0
MASKED_SCORE = -1e30


def layout(lengths):
    segment_ends = jnp.cumsum(lengths, axis=-1)
    segment_starts = segment_ends - lengths
    places = jnp.arange(SEQ, dtype=jnp.int32)
    segment = jnp.sum((places[:, None] >= segment_ends[..., None, :]).astype(jnp.int32), axis=-1)
    choose = segment[..., None] == jnp.arange(NSEG, dtype=jnp.int32)
    picked = jnp.sum(jnp.where(choose, segment_starts[..., None, :], 0), axis=-1)
    return (segment, places - picked)


def angles(position):
    frequency = jnp.exp(-(math.log(THETA) * 2.0 / HD) * jnp.arange(HD // 2, dtype=jnp.float32))
    phase_angle = position.astype(jnp.float32)[..., None] * frequency
    phase_angle = jnp.concatenate([phase_angle, phase_angle], axis=-1)
    return (jnp.cos(phase_angle), jnp.sin(phase_angle))


def plain_dot(left_side, right_side):
    return jnp.dot(left_side, right_side, preferred_element_type=jnp.float32)


def trans_dot(left_side, right_side):
    return lax.dot_general(
        left_side, right_side, (((1,), (1,)), ((), ())), preferred_element_type=jnp.float32
    )


def outer_dot(left_side, right_side):
    return lax.dot_general(
        left_side, right_side, (((0,), (0,)), ((), ())), preferred_element_type=jnp.float32
    )


BLOCK = 256


def rotated(values, cosine, signed_sine):
    return values * cosine + pltpu.roll(values, HD // 2, 1) * signed_sine


def unrotated(values, cosine, signed_sine):
    return values * cosine - pltpu.roll(values, HD // 2, 1) * signed_sine


def allowed_block(start, top, width):
    row = top + lax.broadcasted_iota(jnp.int32, (BLOCK, width), 0)
    col = lax.broadcasted_iota(jnp.int32, (BLOCK, width), 1)
    return (col >= start) & (col <= row)


def attend_body(
    q_pre, k_pre, v_pre, cosine, signed_sine, start, q_out, k_out, v_out, att_out, lse_out
):
    head = pl.program_id(0)

    @pl.when(head == 0)
    def _():
        k_out[...] = rotated(k_pre[...], cosine[...], signed_sine[...]).astype(jnp.bfloat16)
        v_out[...] = v_pre[...].astype(jnp.bfloat16)
        lse_out[...] = jnp.zeros_like(lse_out)

    q_out[...] = rotated(q_pre[...], cosine[...], signed_sine[...]).astype(jnp.bfloat16)
    for top in range(0, SEQ, BLOCK):
        width = top + BLOCK
        rows = pl.ds(top, BLOCK)
        scores = trans_dot(q_out[rows, :], k_out[:width, :]) * HD ** (-0.5)
        scores = jnp.where(allowed_block(start[rows, :], top, width), scores, MASKED_SCORE)
        row_max = jnp.max(scores, axis=1, keepdims=True)
        terms = jnp.exp(scores - row_max)
        total = jnp.sum(terms, axis=1, keepdims=True)
        probs = (terms * (1.0 / total)).astype(jnp.bfloat16)
        att_out[rows, :] = plain_dot(probs, v_out[:width, :]).astype(jnp.bfloat16)
        lane = lax.broadcasted_iota(jnp.int32, (BLOCK, HD), 1)
        lse_out[rows, :] = jnp.where(lane == head, row_max + jnp.log(total), lse_out[rows, :])


def attend_back_body(
    q_rot, k_rot, v_low, d_att, lse, cosine, signed_sine, start, grad_out, dk_sum, dv_sum
):
    head = pl.program_id(0)

    @pl.when(head == 0)
    def _():
        dk_sum[...] = jnp.zeros_like(dk_sum)
        dv_sum[...] = jnp.zeros_like(dv_sum)

    for top in range(0, SEQ, BLOCK):
        width = top + BLOCK
        rows = pl.ds(top, BLOCK)
        query = q_rot[rows, :]
        d_out = d_att[rows, :]
        lane = lax.broadcasted_iota(jnp.int32, (BLOCK, HD), 1)
        row_lse = jnp.sum(jnp.where(lane == head, lse[rows, :], 0.0), axis=1, keepdims=True)
        scores = trans_dot(query, k_rot[:width, :]) * HD ** (-0.5)
        scores = jnp.where(allowed_block(start[rows, :], top, width), scores, MASKED_SCORE)
        probs = jnp.exp(scores - row_lse)
        d_probs = trans_dot(d_out, v_low[:width, :])
        inner = jnp.sum(probs * d_probs, axis=1, keepdims=True)
        d_scores = (probs * (d_probs - inner)).astype(jnp.bfloat16)
        d_query = plain_dot(d_scores, k_rot[:width, :]) * HD ** (-0.5)
        d_query = unrotated(d_query, cosine[rows, :], signed_sine[rows, :])
        cols = pl.ds(pl.multiple_of(head * HD, HD), HD)
        grad_out[rows, cols] = d_query.astype(jnp.bfloat16)
        dk_sum[:width, :] += outer_dot(d_scores, query)
        dv_sum[:width, :] += outer_dot(probs.astype(jnp.bfloat16), d_out)

    @pl.when(head == pl.num_programs(0) - 1)
    def _():
        edge = grad_out.shape[1] - 2 * HD
        d_key = unrotated(dk_sum[...] * HD ** (-0.5), cosine[...], signed_sine[...])
        grad_out[:, edge : edge + HD] = d_key.astype(jnp.bfloat16)
        grad_out[:, edge + HD :] = dv_sum[...].astype(jnp.bfloat16)


def fixed(shape):
    return pl.BlockSpec(shape, lambda head: (0, 0))


def column(index):
    return pl.BlockSpec((SEQ, HD), lambda head: (0, index))


PER_HEAD = pl.BlockSpec((SEQ, HD), lambda head: (0, head))
WHOLE = (SEQ, HD)


def attend(qkv_pre, cosine, signed_sine, start):
    heads = qkv_pre.shape[1] // HD - 2
    shape = lambda cols, kind: jax.ShapeDtypeStruct((SEQ, cols), kind)
    low = jnp.bfloat16
    return pl.pallas_call(
        attend_body,
        grid=(heads,),
        in_specs=[PER_HEAD, column(heads), column(heads + 1)]
        + [fixed(WHOLE), fixed(WHOLE), fixed((SEQ, 1))],
        out_specs=[PER_HEAD, fixed(WHOLE), fixed(WHOLE), PER_HEAD, fixed(WHOLE)],
        out_shape=[
            shape(heads * HD, low),
            shape(HD, low),
            shape(HD, low),
            shape(heads * HD, low),
            shape(HD, jnp.float32),
        ],
    )(qkv_pre, qkv_pre, qkv_pre, cosine, signed_sine, start)


def attend_back(q_rot, k_rot, v_low, d_att, lse, cosine, signed_sine, start):
    heads = q_rot.shape[1] // HD
    cols = (heads + 2) * HD
    return pl.pallas_call(
        attend_back_body,
        grid=(heads,),
        in_specs=[PER_HEAD, fixed(WHOLE), fixed(WHOLE), PER_HEAD, fixed(WHOLE)]
        + [fixed(WHOLE), fixed(WHOLE), fixed((SEQ, 1))],
        out_specs=fixed((SEQ, cols)),
        out_shape=jax.ShapeDtypeStruct((SEQ, cols), jnp.bfloat16),
        scratch_shapes=[pltpu.VMEM(WHOLE, jnp.float32), pltpu.VMEM(WHOLE, jnp.float32)],
    )(q_rot, k_rot, v_low, d_att, lse, cosine, signed_sine, start)


AXES = ("group", "dp", "tensor")


def routes(dp_count):
    def table(move):
        flat = lambda g, d, t: (g * dp_count + d) * 2 + t
        return [
            (flat(g, d, t), flat(*move(g, d, t)))
            for g in range(2)
            for d in range(dp_count)
            for t in range(2)
        ]

    shifts = {
        step: table(lambda g, d, t: (g, (d + 2 * step) % dp_count, t))
        for step in range(1, dp_count // 2)
    }
    return shifts | {
        "x": table(lambda g, d, t: (g, d ^ 1, t)),
        "y": table(lambda g, d, t: (g ^ 1, d, t)),
        "t": table(lambda g, d, t: (g, d, t ^ 1)),
        "first": table(lambda g, d, t: (g, d ^ 1, t) if t == 0 else (g ^ 1, d, t)),
        "second": table(lambda g, d, t: (g ^ 1, d, t) if t == 0 else (g, d ^ 1, t)),
    }


def layer(
    inputs,
    cotangent,
    lengths,
    attn_gain,
    w_query,
    b_query,
    w_key,
    b_key,
    w_value,
    b_value,
    w_out,
    ffn_gain,
    w_gate,
    w_up,
    w_down,
):
    bf16 = jnp.bfloat16
    f32 = jnp.float32
    dp_count = lax.axis_size("dp")
    line = dp_count // 2
    dp_index = lax.axis_index("dp")
    x_index = dp_index % 2
    z_index = dp_index // 2
    y_index = lax.axis_index("group")
    core = lax.axis_index("tensor")
    table = routes(dp_count)
    line_groups = [[2 * z + x for z in range(line)] for x in range(2)]
    tokens, d_model = inputs.shape
    half = tokens // 2
    rows = w_query.shape[0]
    head_count = w_query.shape[1] // HD
    kv_count = w_key.shape[1] // HD
    ffn_cols = w_gate.shape[1]
    quarter = -(-ffn_cols // 512) * 128

    def send(value, route):
        return lax.ppermute(value, AXES, table[route])

    def pick(value, index):
        return lax.dynamic_index_in_dim(value, index, 0, keepdims=False)

    def in_order(index, mine, other):
        first = index == 0
        return jnp.where(first, mine, other), jnp.where(first, other, mine)

    def my_half(value):
        return pick(value.reshape(2, half, value.shape[-1]), core)

    def other_half(value):
        return pick(value.reshape(2, half, value.shape[-1]), 1 - core)

    def both_halves(mine):
        return jnp.concatenate(in_order(core, mine, send(mine, "t")), axis=0)

    def after(value, *others):
        return lax.optimization_barrier((value, *others))[0]

    def square_far(mine, near, *others):
        mine_sib = send(mine, "t")
        near_sib = send(near, "t")
        far = send(after(jnp.stack([mine, near]), *others), "second")
        far_sib = send(far, "t")
        whole = jnp.concatenate(
            [mine, near, far[0], far[1], mine_sib, near_sib, far_sib[0], far_sib[1]], axis=0
        )
        return whole, far

    def scatter_far(mine, theirs):
        came = send(theirs, "t")
        total = (mine.astype(f32) + came.astype(f32)).reshape(4, half, d_model)
        return total[:2], send(total[2:].astype(bf16), "second")

    def scatter_near(kept, came):
        total = kept + came.astype(f32)
        came = send(total[1].astype(bf16), "first")
        return total[0] + came.astype(f32)

    def ffn_quarter(weight, index):
        parts = [weight[:, i * quarter : (i + 1) * quarter] for i in range(4)]
        parts[3] = jnp.pad(parts[3], ((0, 0), (0, 4 * quarter - ffn_cols)))
        upper = jnp.where(index % 2 == 0, parts[2], parts[3])
        lower = jnp.where(index % 2 == 0, parts[0], parts[1])
        return jnp.where(index < 2, lower, upper)

    def ffn_pair(weights):
        other = [ffn_quarter(w, (1 - x_index) * 2 + y_index) for w in weights]
        came = send(jnp.concatenate(other, axis=1), "x")
        mine = [ffn_quarter(w, x_index * 2 + y_index) for w in weights]
        return jnp.stack(in_order(x_index, jnp.concatenate(mine, axis=1), came))

    def ffn_gather(pair):
        full = lax.all_gather(pair, "dp", axis=0, axis_index_groups=line_groups)
        return full.reshape(d_model, pair.shape[-1])

    def ffn_scatter(grad):
        parts = grad.astype(bf16).reshape(line, 2 * rows, quarter)
        return lax.psum_scatter(
            parts, "dp", scatter_dimension=0, axis_index_groups=line_groups
        ).reshape(2, rows, quarter)

    def ffn_swap(summed, *others):
        came = send(pick(summed, 1 - x_index), "x")
        pair = jnp.stack(in_order(x_index, pick(summed, x_index), came))
        low, high = in_order(y_index, pair, send(after(pair, *others), "y"))
        whole = jnp.concatenate([low[0], high[0], low[1], high[1]], axis=1)
        return whole[:, :ffn_cols].astype(f32)

    cut = line // 2
    part_rows = rows // 2

    def line_sends(weight):
        mine = lax.dynamic_slice_in_dim(weight, y_index * part_rows, part_rows, 0)
        return [mine] + [send(mine, step) for step in range(1, line)]

    def line_join(pieces):
        whole = jnp.zeros((line,) + pieces[0].shape, bf16)
        for step, piece in enumerate(pieces):
            spot = ((z_index - step) % line, 0, 0)
            whole = lax.dynamic_update_slice(whole, piece[None], spot)
        return whole

    def near_sends(blocks):
        low, high = blocks[:cut], blocks[cut:]
        return low, high, send(low, "x"), send(high, "y")

    def far_join(low, high, low_near, high_near):
        low_far = send(jnp.stack([low, low_near]), "y")
        high_far = send(jnp.stack([high, high_near]), "x")
        cols = low.shape[-1]
        whole = jnp.zeros((line, 2, 2, part_rows, cols), bf16)
        x, y = x_index, y_index
        for piece, z, px, py in (
            (low, 0, x, y),
            (low_near, 0, 1 - x, y),
            (low_far[0], 0, x, 1 - y),
            (low_far[1], 0, 1 - x, 1 - y),
            (high, cut, x, y),
            (high_near, cut, x, 1 - y),
            (high_far[0], cut, 1 - x, y),
            (high_far[1], cut, 1 - x, 1 - y),
        ):
            whole = lax.dynamic_update_slice(whole, piece[:, None, None], (z, px, py, 0, 0))
        return whole.reshape(d_model, cols)

    def take(value, axis, index):
        return lax.dynamic_index_in_dim(value, index, axis, keepdims=False)

    def fold(value, axis, index, route):
        came = send(take(value, axis, 1 - index), route)
        return (take(value, axis, index).astype(f32) + came.astype(f32)).astype(bf16)

    def scatter_hop1(grad):
        view = grad.reshape(line, 2, 2, part_rows, grad.shape[-1])
        low = fold(view[:cut], 1, x_index, "x")
        return low, fold(view[cut:], 2, y_index, "y")

    def scatter_hop2(low, high):
        return jnp.concatenate([fold(low, 1, y_index, "y"), fold(high, 1, x_index, "x")])

    def scatter_line(blocks):
        total = pick(blocks, z_index).astype(f32)
        for step in range(1, line):
            total = total + send(pick(blocks, (z_index + step) % line), step).astype(f32)
        return total.astype(bf16)

    def scatter_end(mine):
        return jnp.concatenate(in_order(y_index, mine, send(mine, "y"))).astype(f32)

    query_cols = head_count * HD
    key_cols = kv_count * HD
    qkv_cols = query_cols + 2 * key_cols
    gains = jnp.pad(jnp.stack([attn_gain, ffn_gain], axis=1), ((0, 0), (0, HD - 2)))

    qkv_pieces = line_sends(jnp.concatenate([w_query, w_key, w_value, gains], axis=1))
    gate_up_pair = ffn_pair([w_gate, w_up])
    gate_up_full = ffn_gather(after(gate_up_pair, *qkv_pieces))
    qkv_near = near_sends(after(line_join(qkv_pieces), gate_up_pair))
    qkv_full = far_join(*qkv_near)
    out_pieces = line_sends(after(w_out, *qkv_near))
    out_near = near_sends(after(line_join(out_pieces), qkv_full))
    out_full = far_join(*out_near)
    down_pair = ffn_pair([after(w_down, out_full)])
    down_full = ffn_gather(after(down_pair, gate_up_pair))
    cot_half = my_half(cotangent)
    cot_near = send(after(cot_half, out_full), "first")

    _, position = layout(lengths[0])
    cosine, sine_table = angles(position)
    sign = jnp.where(jnp.arange(HD) < HD // 2, -1.0, 1.0)
    signed_sine = sine_table * sign
    start = (jnp.arange(SEQ, dtype=jnp.int32) - position)[:, None]
    stream = inputs.astype(f32)
    inv_one = lax.rsqrt(jnp.mean(stream * stream, axis=-1, keepdims=True) + EPSILON)
    qkv_full = after(qkv_full, cosine, signed_sine, start, inv_one)
    gain_one = qkv_full[:, qkv_cols].astype(f32)
    gain_two = qkv_full[:, qkv_cols + 1].astype(f32)
    qkv_full = qkv_full[:, :qkv_cols]

    h_one = (stream * inv_one * gain_one).astype(bf16)
    qkv_bias = jnp.concatenate([b_query, b_key, b_value]).astype(f32)
    qkv_pre = plain_dot(h_one, qkv_full) + qkv_bias
    q_rot, k_rot, v_low, attended, lse = attend(
        after(qkv_pre, *out_near), cosine, signed_sine, start
    )
    branch = trans_dot(attended, out_full)
    resid = (
        my_half(stream)
        + my_half(branch)
        + send(other_half(branch).astype(bf16), "t").astype(f32)
    )
    inv_two = lax.rsqrt(jnp.mean(resid * resid, axis=-1, keepdims=True) + EPSILON)
    norm_two = resid * inv_two
    h_two_half = after((norm_two * gain_two).astype(bf16), cot_near)
    h_two, h_two_far = square_far(h_two_half, send(h_two_half, "first"))
    cot_all, _ = square_far(cot_half, cot_near, h_two_far)

    gate_full = gate_up_full[:, :quarter]
    up_full = gate_up_full[:, quarter:]
    gate_low = plain_dot(h_two, gate_full).astype(bf16)
    up_low = plain_dot(after(h_two, gate_low), up_full).astype(bf16)
    gate_pre = gate_low.astype(f32)
    up_pre = up_low.astype(f32)
    sigmoid_gate = jax.nn.sigmoid(gate_pre)
    swish_gate = gate_pre * sigmoid_gate
    hidden = (swish_gate * up_pre).astype(bf16)
    down_part = outer_dot(cot_all, hidden).astype(bf16)
    down_sum = ffn_scatter(down_part)
    d_hidden = plain_dot(after(cot_all, down_part), down_full)
    d_gate = (d_hidden * up_pre * sigmoid_gate * (1.0 + gate_pre * (1.0 - sigmoid_gate))).astype(
        bf16
    )
    d_up = (d_hidden * swish_gate).astype(bf16)
    mid = 4 * half
    low_hidden = after(hidden, d_gate)
    ffn_theirs = trans_dot(low_hidden[mid:], down_full).astype(bf16)
    gate_part = outer_dot(after(h_two, ffn_theirs), d_gate).astype(bf16)
    gate_sum = ffn_scatter(gate_part)
    ffn_mine = trans_dot(after(low_hidden[:mid], gate_part), down_full).astype(bf16)
    ffn_kept, ffn_came = scatter_far(ffn_mine, ffn_theirs)

    def entry(gate_side, up_side):
        return (trans_dot(gate_side, gate_full) + trans_dot(up_side, up_full)).astype(bf16)

    theirs = entry(after(d_gate[mid:], ffn_mine), after(d_up[mid:], ffn_mine))
    mine = entry(after(d_gate[:mid], theirs), after(d_up[:mid], theirs))
    kept, came = scatter_far(mine, theirs)
    up_part = outer_dot(after(h_two, mine), d_up).astype(bf16)
    up_sum = ffn_scatter(up_part)
    d_h_two = scatter_near(kept, after(came, up_part))
    ffn_total = scatter_near(ffn_kept, after(ffn_came, d_h_two))
    layer_out = both_halves((resid + ffn_total).astype(bf16))

    scaled = d_h_two * gain_two
    d_resid = cot_half.astype(f32) + inv_two * (
        scaled - norm_two * jnp.mean(norm_two * scaled, axis=-1, keepdims=True)
    )
    gain_two_part = jnp.sum(d_h_two * norm_two, axis=0)
    d_out_low = both_halves(d_resid.astype(bf16))
    out_hop = scatter_hop1(outer_dot(d_out_low, attended).astype(bf16))
    down_grad = ffn_swap(down_sum)
    d_attended = plain_dot(d_out_low, out_full).astype(bf16)
    d_qkv = attend_back(q_rot, k_rot, v_low, d_attended, lse, cosine, signed_sine, start)
    qkv_part = outer_dot(after(h_one, *out_hop), d_qkv).astype(bf16)
    qkv_hop = scatter_hop1(qkv_part)
    out_blocks = scatter_hop2(*out_hop)
    qkv_blocks = scatter_hop2(*qkv_hop)
    out_mine = scatter_line(out_blocks)
    qkv_mine = scatter_line(after(qkv_blocks, out_mine))
    out_grad = scatter_end(out_mine)
    qkv_grad = scatter_end(qkv_mine)
    gate_grad = ffn_swap(after(gate_sum, d_out_low), *qkv_hop)
    entry_one = trans_dot(d_qkv, qkv_full)
    d_h_one = my_half(entry_one) + send(other_half(entry_one).astype(bf16), "t").astype(f32)
    half_inv = my_half(inv_one)
    norm_one = my_half(stream) * half_inv
    scaled = d_h_one * gain_one
    input_grad = both_halves(
        (
            d_resid
            + half_inv * (scaled - norm_one * jnp.mean(norm_one * scaled, axis=-1, keepdims=True))
        ).astype(bf16)
    )
    gain_one_part = jnp.sum(d_h_one * norm_one, axis=0)

    bias_part = jnp.sum(d_qkv.astype(f32), axis=0)
    small = jnp.concatenate([gain_one_part, gain_two_part, bias_part]).reshape(-1, 128)
    small = small + send(small, "y")
    step = 1
    while step < dp_count:
        small = small + lax.ppermute(small, "dp", [(i, i ^ step) for i in range(dp_count)])
        step *= 2
    small = small.reshape(-1)
    up_grad = ffn_swap(after(up_sum, gate_grad, qkv_mine, small))
    gain_sums = small[: 2 * d_model].reshape(2, dp_count, rows)
    gain_mine = lax.dynamic_index_in_dim(gain_sums, dp_index, 1, keepdims=False)
    gain_mine = gain_mine + send(gain_mine, "t")
    bias_sum = small[2 * d_model :]
    return (
        layer_out,
        input_grad,
        gain_mine[0],
        qkv_grad[:, :query_cols],
        bias_sum[:query_cols],
        qkv_grad[:, query_cols : query_cols + key_cols],
        bias_sum[query_cols : query_cols + key_cols],
        qkv_grad[:, query_cols + key_cols :],
        bias_sum[query_cols + key_cols :],
        out_grad,
        gain_mine[1],
        gate_grad,
        up_grad,
        down_grad,
    )


def solution(mesh):
    in_specs = (
        P(("group", "dp"), None),
        P(("group", "dp"), None),
        P(("group", "dp"), None),
        P("dp"),
        P("dp", "tensor"),
        P("tensor"),
        P("dp", "tensor"),
        P("tensor"),
        P("dp", "tensor"),
        P("tensor"),
        P("dp", "tensor"),
        P("dp"),
        P("dp", "tensor"),
        P("dp", "tensor"),
        P("dp", "tensor"),
    )
    out_specs = (
        P(("group", "dp"), None),
        P(("group", "dp"), None),
        P("dp"),
        P("dp", "tensor"),
        P("tensor"),
        P("dp", "tensor"),
        P("tensor"),
        P("dp", "tensor"),
        P("tensor"),
        P("dp", "tensor"),
        P("dp"),
        P("dp", "tensor"),
        P("dp", "tensor"),
        P("dp", "tensor"),
    )
    return jax.shard_map(layer, mesh=mesh, in_specs=in_specs, out_specs=out_specs, check_vma=False)
```

profile of v0, /device:TPU:0, one launch (start us, length us, event | category | flops | bytes accessed | tf_op | source)
XLA Modules:
  0.0 703.6 jit_solution(9321730467922123935)
XLA Ops:
  32.5 12.0 %collective-permute-done.3 = bf16[192,2304]{1,0:T(8,128)(2,1)} collective-permute-done((bf16[192,2304]{1,0:T(8,128)(2,1)}, bf16[192,2304]{1,0:T(8,128)(2,1)}, u32[]{:S(2)}, u32[]{:S(2)}) %collective-permute-start.3) | collective-permute-done | bytes 884768 | tf_op jit(solution)/shard_map/ppermute | solution.py:243
  65.6 9.9 %collective-permute-done.8 = bf16[96,768]{1,0:T(8,128)(2,1)S(1)} collective-permute-done((bf16[96,768]{1,0:T(8,128)(2,1)S(1)}, bf16[96,768]{1,0:T(8,128)(2,1)S(1)}, u32[]{:S(2)}, u32[]{:S(2)}) %collective-permute-start.8) | collective-permute-done | bytes 147488 | tf_op jit(solution)/shard_map/ppermute | solution.py:243
  96.8 13.0 %shard_map.254 = (bf16[768,768]{1,0:T(8,128)(2,1)}, bf16[768,128]{1,0:T(8,128)(2,1)}, bf16[768,128]{1,0:T(8,128)(2,1)}, bf16[768,768]{1,0:T(8,128)(2,1)}, f32[768,128]{1,0:T(8,128)}) custom-call(f32[768,1024]{1,0:T(8,128)} %fusion.29.q_pre.k_pre.v_pre, f32[768,1024]{1,0:T(8,128)} %fusion.29.q_pre.k_pre.v_pre, f32[768,1024]{1,0:T(8,128)} %fusion.29.q_pre.k_pre.v_pre, ...), custom_call_target="tpu_custom_call" | custom-call | tf_op jit(solution)/shard_map/pallas_call | solution.py:150
  145.2 15.5 %collective-permute-done.17 = bf16[384,1536]{1,0:T(8,128)(2,1)S(1)} collective-permute-done((bf16[384,1536]{1,0:T(8,128)(2,1)S(1)}, bf16[384,1536]{1,0:T(8,128)(2,1)S(1)}, u32[]{:S(2)}, u32[]{:S(2)}) %collective-permute-start.17) | collective-permute-done | bytes 1179680 | tf_op jit(solution)/shard_map/ppermute | solution.py:243
  165.3 12.3 %collective-permute-done.26 = bf16[192,1152]{1,0:T(8,128)(2,1)S(1)} collective-permute-done((bf16[192,1152]{1,0:T(8,128)(2,1)S(1)}, bf16[192,1152]{1,0:T(8,128)(2,1)S(1)}, u32[]{:S(2)}, u32[]{:S(2)}) %collective-permute-start.26) | collective-permute-done | bytes 442400 | tf_op jit(solution)/shard_map/ppermute | solution.py:243
  179.1 21.4 %collective-permute-start.19 = (bf16[384,1536]{1,0:T(8,128)(2,1)S(1)}, bf16[384,1536]{1,0:T(8,128)(2,1)S(1)}, u32[]{:S(2)}, u32[]{:S(2)}) collective-permute-start(bf16[384,1536]{1,0:T(8,128)(2,1)S(1)} %multiply_convert_fusion.2), channel_id=1, source_target_pairs={{0,1},{1,0},{2,3},{3,2},{4,5},{5,4},{6,7},{7,6},{8,9},{9,8},{10,11... | collective-permute-start | bytes 3538952 | tf_op jit(solution)/shard_map/ppermute | solution.py:243
  207.3 22.4 %collective-permute-done.22 = bf16[2,384,1536]{2,1,0:T(8,128)(2,1)} collective-permute-done((bf16[2,384,1536]{2,1,0:T(8,128)(2,1)S(1)}, bf16[2,384,1536]{2,1,0:T(8,128)(2,1)}, u32[]{:S(2)}, u32[]{:S(2)}) %collective-permute-start.22) | collective-permute-done | bytes 2359328 | tf_op jit(solution)/shard_map/ppermute | solution.py:243
  241.8 18.3 %convolution_convert_fusion.1 = bf16[3072,1152]{1,0:T(8,128)(2,1)} fusion(bf16[3072,1536]{1,0:T(8,128)(2,1)} %copy-done.44, bf16[1536,2304]{1,0:T(8,128)(2,1)} %bitcast.445), kind=kOutput, calls=%fused_computation.15 | convolution fusion | flops 10875174912 | bytes 20054016 | tf_op jit(solution)/shard_map/dot_general | solution.py:38
  260.1 20.4 %fusion = (bf16[3072,1152]{1,0:T(8,128)(2,1)S(1)}, bf16[3072,1152]{1,0:T(8,128)(2,1)}) fusion(bf16[3072,1152]{1,0:T(8,128)(2,1)} %convolution_convert_fusion.1, bf16[3072,1536]{1,0:T(8,128)(2,1)} %copy-done.44, bf16[1536,2304]{1,0:T(8,128)(2,1)} %bitcast.446), kind=kOutput, calls=%fused_computation.5 | convolution fusion | flops 10903486464 | bytes 34209792 | tf_op jit(solution)/shard_map/dot_general | solution.py:38
  286.1 16.3 %convolution_convert_fusion.6 = bf16[1536,1152]{1,0:T(8,128)(2,1)} fusion(bf16[3072,1536]{1,0:T(8,128)(2,1)} %fusion.38, bf16[3072,1152]{1,0:T(8,128)(2,1)S(1)} %get-tuple-element.61), kind=kOutput, calls=%fused_computation.24 | convolution fusion | flops 10873405440 | bytes 20054016 | tf_op jit(solution)/shard_map/dot_general | solution.py:48
  302.5 26.4 %multiply_convert_fusion = (bf16[3072,1152]{1,0:T(8,128)(2,1)}, bf16[3072,1152]{1,0:T(8,128)(2,1)}) fusion(bf16[3072,1152]{1,0:T(8,128)(2,1)} %convolution_convert_fusion.1, bf16[3072,1152]{1,0:T(8,128)(2,1)} %get-tuple-element.180, bf16[3072,1536]{1,0:T(8,128)(2,1)} %fusion.38, bf16[1536,1152]{1,0:T(8,128)(2,1)} %bitcast.453), kind=kOutput, calls=%fused_computation.13 | convolution fusion | flops 10924720128 | bytes 41287680 | tf_op jit(solution)/shard_map/dot_general | solution.py:38
  328.9 10.2 %convolution_convert_fusion.3 = bf16[1536,1536]{1,0:T(8,128)(2,1)} fusion(bf16[1536,1152]{1,0:T(8,128)(2,1)S(1)} %bitcast.455, bf16[3072,1152]{1,0:T(8,128)(2,1)} %copy-done.34), kind=kOutput, calls=%fused_computation.21 | convolution fusion | flops 5438177280 | bytes 11796480 | tf_op jit(solution)/shard_map/dot_general | solution.py:42
  343.4 16.5 %convolution_convert_fusion.5 = bf16[1536,1152]{1,0:T(8,128)(2,1)} fusion(bf16[3072,1536]{1,0:T(8,128)(2,1)} %copy-done.44, bf16[3072,1152]{1,0:T(8,128)(2,1)S(1)} %copy-done.10), kind=kOutput, calls=%fused_computation.23 | convolution fusion | flops 10873405440 | bytes 20054016 | tf_op jit(solution)/shard_map/dot_general | solution.py:48
  367.8 11.3 %convert_add_fusion.1 = f32[1536,1536]{1,0:T(8,128)} fusion(bf16[1536,1536]{1,0:T(8,128)(2,1)} %collective-permute-done.27, bf16[1536,1152]{1,0:T(8,128)(2,1)S(1)} %copy-done.24, bf16[1536,1152]{1,0:T(8,128)(2,1)} %bitcast.454), kind=kOutput, calls=%fused_computation.19 | convolution fusion | flops 5445255168 | bytes 21233664 | tf_op jit(solution)/shard_map/dot_general | solution.py:42
  387.9 10.5 %add_convert_fusion.1 = bf16[1536,1536]{1,0:T(8,128)(2,1)} fusion(f32[1536,1536]{1,0:T(8,128)} %fusion.18, bf16[1536,1152]{1,0:T(8,128)(2,1)S(1)} %get-tuple-element.65, bf16[1536,2304]{1,0:T(8,128)(2,1)S(1)} %bitcast.452), kind=kOutput, calls=%fused_computation.18 | convolution fusion | flops 5440536576 | bytes 21233664 | tf_op jit(solution)/shard_map/dot_general | solution.py:42
  407.8 11.3 %fusion.16 = f32[1536,1536]{1,0:T(8,128)} fusion(bf16[1536,1152]{1,0:T(8,128)(2,1)} %get-tuple-element.66, bf16[1536,2304]{1,0:T(8,128)(2,1)} %bitcast.447), kind=kOutput, calls=%fused_computation.42 | convolution fusion | flops 5435817984 | bytes 16515072 | tf_op jit(solution)/shard_map/dot_general | solution.py:42
  419.1 22.1 %reduce-scatter.4.cloned.1.call-done = bf16[1,384,1152]{2,1,0:T(8,128)(2,1)} async-done(((bf16[4,384,1152]{2,1,0:T(8,128)(2,1)}), bf16[1,384,1152]{2,1,0:T(8,128)(2,1)}) %reduce-scatter.4.cloned.1.call-update) | async-done | bytes 884752 | tf_op jit(solution)/shard_map/reduce_scatter | solution.py:303
  455.3 10.5 %convert_add_fusion = f32[1536,1536]{1,0:T(8,128)S(1)} fusion(bf16[1536,1536]{1,0:T(8,128)(2,1)} %collective-permute-done.29, f32[1536,1536]{1,0:T(8,128)} %fusion.16, bf16[1536,1152]{1,0:T(8,128)(2,1)S(1)} %get-tuple-element.67, bf16[1536,2304]{1,0:T(8,128)(2,1)} %bitcast.448), kind=kOutput, calls=%fused_computation.16 | convolution fusion | flops 5447614464 | bytes 30670848 | tf_op jit(solution)/shard_map/dot_general | solution.py:42
  470.8 16.0 %convolution_convert_fusion.4 = bf16[1536,1152]{1,0:T(8,128)(2,1)} fusion(bf16[3072,1536]{1,0:T(8,128)(2,1)} %copy-done.44, bf16[3072,1152]{1,0:T(8,128)(2,1)S(1)} %bitcast.414), kind=kOutput, calls=%fused_computation.22 | convolution fusion | flops 10873405440 | bytes 20054016 | tf_op jit(solution)/shard_map/dot_general | solution.py:48
  501.0 12.8 %collective-permute-done.31 = bf16[384,1536]{1,0:T(8,128)(2,1)} collective-permute-done((bf16[384,1536]{1,0:T(8,128)(2,1)}, bf16[384,1536]{1,0:T(8,128)(2,1)}, u32[]{:S(2)}, u32[]{:S(2)}) %collective-permute-start.31) | collective-permute-done | bytes 1179680 | tf_op jit(solution)/shard_map/ppermute | solution.py:243
  537.4 16.8 %shard_map.255 = bf16[768,1024]{1,0:T(8,128)(2,1)} custom-call(bf16[768,768]{1,0:T(8,128)(2,1)} %get-tuple-element.71.q_rot, bf16[768,128]{1,0:T(8,128)(2,1)} %get-tuple-element.72.k_rot, bf16[768,128]{1,0:T(8,128)(2,1)} %get-tuple-element.73.v_low, bf16[768,768]{1,0:T(8,128)(2,1)} %convolution_convert_fusion.9.d_att, f32[768,128]{1,0:T(8,128)} %get-tuple-element.74.lse, ...), custom_call_target="tpu_custom_call" | custom-call | tf_op jit(solution)/shard_map/pallas_call | solution.py:169
  589.7 11.4 %collective-permute-done.37 = f32[32,128]{1,0:T(8,128)S(1)} collective-permute-done((f32[32,128]{1,0:T(8,128)S(1)}, f32[32,128]{1,0:T(8,128)S(1)}, u32[]{:S(2)}, u32[]{:S(2)}) %collective-permute-start.37) | collective-permute-done | bytes 16416 | tf_op jit(solution)/shard_map/ppermute | solution.py:243
  653.5 10.8 %collective-permute-done.56 = bf16[96,1024]{1,0:T(8,128)(2,1)S(1)} collective-permute-done((bf16[96,1024]{1,0:T(8,128)(2,1)S(1)}, bf16[96,1024]{1,0:T(8,128)(2,1)S(1)}, u32[]{:S(2)}, u32[]{:S(2)}) %collective-permute-start.56) | collective-permute-done | bytes 196640 | tf_op jit(solution)/shard_map/ppermute | solution.py:243
  682.2 12.3 %collective-permute-done.61 = bf16[2,192,1152]{2,1,0:T(8,128)(2,1)S(1)} collective-permute-done((bf16[2,192,1152]{2,1,0:T(8,128)(2,1)S(1)}, bf16[2,192,1152]{2,1,0:T(8,128)(2,1)S(1)}, u32[]{:S(2)}, u32[]{:S(2)}) %collective-permute-start.61) | collective-permute-done | bytes 884768 | tf_op jit(solution)/shard_map/ppermute | solution.py:243
  (466 shorter events, 327.6 us)
Async XLA Ops:
  7.2 234.6 %all-gather.5.cloned.1.call-start = ((), (), s32[]{:S(2)}) async-start(), calls=%async_computation.6 | async-start | bytes 8847360 | tf_op jit(solution)/shard_map/all_gather | solution.py:298
  47.3 255.2 %all-gather.7.cloned.1.call-start = ((), (), s32[]{:S(2)}) async-start(), calls=%async_computation.7 | async-start | bytes 4423680 | tf_op jit(solution)/shard_map/all_gather | solution.py:298
  162.5 38.2 %collective-permute-start.18 = (bf16[2,384,1536]{2,1,0:T(8,128)(2,1)}, bf16[2,384,1536]{2,1,0:T(8,128)(2,1)}, u32[]{:S(2)}, u32[]{:S(2)}) collective-permute-start(bf16[2,384,1536]{2,1,0:T(8,128)(2,1)} %pad_maximum_fusion), channel_id=1, source_target_pairs={{0,16},{1,3},{2,18},{3,1},{4,20},{5,7},{6,22},{7,5},{8,24},{9,11},... | collective-permute-start | bytes 7077896 | tf_op jit(solution)/shard_map/ppermute | solution.py:243
  165.3 69.2 %collective-permute-start.23 = (bf16[384,1536]{1,0:T(8,128)(2,1)S(1)}, bf16[384,1536]{1,0:T(8,128)(2,1)}, u32[]{:S(2)}, u32[]{:S(2)}) collective-permute-start(bf16[384,1536]{1,0:T(8,128)(2,1)S(1)} %bitcast.406), channel_id=1, source_target_pairs={{0,1},{1,0},{2,3},{3,2},{4,5},{5,4},{6,7},{7,6},{8,9},{9,8},{10,11... | collective-permute-start | bytes 3538952 | tf_op jit(solution)/shard_map/ppermute | solution.py:243
  179.0 226.3 %reduce-scatter.8.cloned.1.call-start = ((), (), s32[]{:S(2)}) async-start(), calls=%async_computation.5 | async-start | bytes 4423680 | tf_op jit(solution)/shard_map/reduce_scatter | solution.py:303
  179.1 28.0 %collective-permute-start.19 = (bf16[384,1536]{1,0:T(8,128)(2,1)S(1)}, bf16[384,1536]{1,0:T(8,128)(2,1)S(1)}, u32[]{:S(2)}, u32[]{:S(2)}) collective-permute-start(bf16[384,1536]{1,0:T(8,128)(2,1)S(1)} %multiply_convert_fusion.2), channel_id=1, source_target_pairs={{0,1},{1,0},{2,3},{3,2},{4,5},{5,4},{6,7},{7,6},{8,9},{9,8},{10,11... | collective-permute-start | bytes 3538952 | tf_op jit(solution)/shard_map/ppermute | solution.py:243
  200.7 29.0 %collective-permute-start.22 = (bf16[2,384,1536]{2,1,0:T(8,128)(2,1)S(1)}, bf16[2,384,1536]{2,1,0:T(8,128)(2,1)}, u32[]{:S(2)}, u32[]{:S(2)}) collective-permute-start(bf16[2,384,1536]{2,1,0:T(8,128)(2,1)S(1)} %pad_maximum_fusion.1), channel_id=1, source_target_pairs={{0,16},{1,3},{2,18},{3,1},{4,20},{5,7},{6,22},{7,5},{8,24},{9,11},... | collective-permute-start | bytes 7077896 | tf_op jit(solution)/shard_map/ppermute | solution.py:243
  203.7 33.1 %collective-permute-start.21 = (bf16[2,384,1536]{2,1,0:T(8,128)(2,1)}, bf16[2,384,1536]{2,1,0:T(8,128)(2,1)S(1)}, u32[]{:S(2)}, u32[]{:S(2)}) collective-permute-start(bf16[2,384,1536]{2,1,0:T(8,128)(2,1)} %collective-permute-done.18), channel_id=1, source_target_pairs={{0,1},{1,0},{2,3},{3,2},{4,5},{5,4},{6,7},{7,6},{8,9},{9,8},{10,11... | collective-permute-start | bytes 7077896 | tf_op jit(solution)/shard_map/ppermute | solution.py:243
  207.0 30.0 %collective-permute-start.24 = (bf16[384,1536]{1,0:T(8,128)(2,1)S(1)}, bf16[384,1536]{1,0:T(8,128)(2,1)S(1)}, u32[]{:S(2)}, u32[]{:S(2)}) collective-permute-start(bf16[384,1536]{1,0:T(8,128)(2,1)S(1)} %copy-done.17), channel_id=1, source_target_pairs={{0,1},{1,0},{2,3},{3,2},{4,5},{5,4},{6,7},{7,6},{8,9},{9,8},{10,11... | collective-permute-start | bytes 3538952 | tf_op jit(solution)/shard_map/ppermute | solution.py:243
  229.7 50.8 %collective-permute-start.25 = (bf16[2,384,1536]{2,1,0:T(8,128)(2,1)}, bf16[2,384,1536]{2,1,0:T(8,128)(2,1)}, u32[]{:S(2)}, u32[]{:S(2)}) collective-permute-start(bf16[2,384,1536]{2,1,0:T(8,128)(2,1)} %collective-permute-done.22), channel_id=1, source_target_pairs={{0,1},{1,0},{2,3},{3,2},{4,5},{5,4},{6,7},{7,6},{8,9},{9,8},{10,11... | collective-permute-start | bytes 7077896 | tf_op jit(solution)/shard_map/ppermute | solution.py:243
  302.4 138.8 %reduce-scatter.4.cloned.1.call-start = ((), (), s32[]{:S(2)}) async-start(), calls=%async_computation.3 | async-start | bytes 4423680 | tf_op jit(solution)/shard_map/reduce_scatter | solution.py:303
  339.1 28.6 %collective-permute-start.27 = (bf16[1536,1536]{1,0:T(8,128)(2,1)}, bf16[1536,1536]{1,0:T(8,128)(2,1)}, u32[]{:S(2)}, u32[]{:S(2)}) collective-permute-start(bf16[1536,1536]{1,0:T(8,128)(2,1)} %convolution_convert_fusion.3), channel_id=1, source_target_pairs={{0,1},{1,0},{2,3},{3,2},{4,5},{5,4},{6,7},{7,6},{8,9},{9,8},{10,11... | collective-permute-start | bytes 14155784 | tf_op jit(solution)/shard_map/ppermute | solution.py:243
  359.9 308.4 %reduce-scatter.6.cloned.1.call-start = ((), (), s32[]{:S(2)}) async-start(), calls=%async_computation.4 | async-start | bytes 4423680 | tf_op jit(solution)/shard_map/reduce_scatter | solution.py:303
  398.4 56.9 %collective-permute-start.29 = (bf16[1536,1536]{1,0:T(8,128)(2,1)}, bf16[1536,1536]{1,0:T(8,128)(2,1)}, u32[]{:S(2)}, u32[]{:S(2)}) collective-permute-start(bf16[1536,1536]{1,0:T(8,128)(2,1)} %add_convert_fusion.1), channel_id=1, source_target_pairs={{0,1},{1,0},{2,3},{3,2},{4,5},{5,4},{6,7},{7,6},{8,9},{9,8},{10,11... | collective-permute-start | bytes 14155784 | tf_op jit(solution)/shard_map/ppermute | solution.py:243
  403.5 113.1 %collective-permute-start.28 = (bf16[2,384,1536]{2,1,0:T(8,128)(2,1)}, bf16[2,384,1536]{2,1,0:T(8,128)(2,1)}, u32[]{:S(2)}, u32[]{:S(2)}) collective-permute-start(bf16[2,384,1536]{2,1,0:T(8,128)(2,1)} %bitcast.73), channel_id=1, source_target_pairs={{0,16},{1,3},{2,18},{3,1},{4,20},{5,7},{6,22},{7,5},{8,24},{9,11},... | collective-permute-start | bytes 7077896 | tf_op jit(solution)/shard_map/ppermute | solution.py:243
  407.1 36.8 %collective-permute-start.62 = (bf16[192,1152]{1,0:T(8,128)(2,1)}, bf16[192,1152]{1,0:T(8,128)(2,1)}, u32[]{:S(2)}, u32[]{:S(2)}) collective-permute-start(bf16[192,1152]{1,0:T(8,128)(2,1)} %dynamic-slice_bitcast_fusion), channel_id=1, source_target_pairs={{0,2},{1,3},{2,0},{3,1},{4,6},{5,7},{6,4},{7,5},{8,10},{9,11},{10,... | collective-permute-start | bytes 1327112 | tf_op jit(solution)/shard_map/ppermute | solution.py:243
  466.1 28.9 %collective-permute-start.30 = (bf16[2,384,1536]{2,1,0:T(8,128)(2,1)S(1)}, bf16[2,384,1536]{2,1,0:T(8,128)(2,1)S(1)}, u32[]{:S(2)}, u32[]{:S(2)}) collective-permute-start(bf16[2,384,1536]{2,1,0:T(8,128)(2,1)S(1)} %bitcast.429), channel_id=1, source_target_pairs={{0,16},{1,3},{2,18},{3,1},{4,20},{5,7},{6,22},{7,5},{8,24},{9,11},... | collective-permute-start | bytes 7077896 | tf_op jit(solution)/shard_map/ppermute | solution.py:243
  523.6 79.1 %collective-permute-start.32 = (bf16[384,1536]{1,0:T(8,128)(2,1)}, bf16[384,1536]{1,0:T(8,128)(2,1)}, u32[]{:S(2)}, u32[]{:S(2)}) collective-permute-start(bf16[384,1536]{1,0:T(8,128)(2,1)} %fusion.37), channel_id=1, source_target_pairs={{0,2},{1,17},{2,0},{3,19},{4,6},{5,21},{6,4},{7,23},{8,10},{9,25},... | collective-permute-start | bytes 3538952 | tf_op jit(solution)/shard_map/ppermute | solution.py:243
  534.5 26.4 %collective-permute-start.42 = (bf16[2,2,96,768]{3,2,0,1:T(8,128)(2,1)}, bf16[2,2,96,768]{3,2,0,1:T(8,128)(2,1)}, u32[]{:S(2)}, u32[]{:S(2)}) collective-permute-start(bf16[2,2,96,768]{3,2,0,1:T(8,128)(2,1)} %bitcast.398), channel_id=1, source_target_pairs={{0,2},{1,3},{2,0},{3,1},{4,6},{5,7},{6,4},{7,5},{8,10},{9,11},{10,... | collective-permute-start | bytes 1769480 | tf_op jit(solution)/shard_map/ppermute | solution.py:243
  559.4 28.2 %collective-permute-start.35 = (bf16[384,1536]{1,0:T(8,128)(2,1)S(1)}, bf16[384,1536]{1,0:T(8,128)(2,1)S(1)}, u32[]{:S(2)}, u32[]{:S(2)}) collective-permute-start(bf16[384,1536]{1,0:T(8,128)(2,1)S(1)} %fusion.35), channel_id=1, source_target_pairs={{0,1},{1,0},{2,3},{3,2},{4,5},{5,4},{6,7},{7,6},{8,9},{9,8},{10,11... | collective-permute-start | bytes 3538952 | tf_op jit(solution)/shard_map/ppermute | solution.py:243
  581.1 35.4 %collective-permute-start.46 = (bf16[2,2,96,1024]{3,2,0,1:T(8,128)(2,1)}, bf16[2,2,96,1024]{3,2,0,1:T(8,128)(2,1)}, u32[]{:S(2)}, u32[]{:S(2)}) collective-permute-start(bf16[2,2,96,1024]{3,2,0,1:T(8,128)(2,1)} %bitcast.395), channel_id=1, source_target_pairs={{0,16},{1,17},{2,18},{3,19},{4,20},{5,21},{6,22},{7,23},{8,24},{9,... | collective-permute-start | bytes 2359304 | tf_op jit(solution)/shard_map/ppermute | solution.py:243
  585.1 33.7 %collective-permute-start.44 = (bf16[2,2,96,1024]{3,2,0,1:T(8,128)(2,1)}, bf16[2,2,96,1024]{3,2,0,1:T(8,128)(2,1)}, u32[]{:S(2)}, u32[]{:S(2)}) collective-permute-start(bf16[2,2,96,1024]{3,2,0,1:T(8,128)(2,1)} %bitcast.396), channel_id=1, source_target_pairs={{0,2},{1,3},{2,0},{3,1},{4,6},{5,7},{6,4},{7,5},{8,10},{9,11},{10,... | collective-permute-start | bytes 2359304 | tf_op jit(solution)/shard_map/ppermute | solution.py:243
  606.8 64.2 %collective-permute-start.36 = (bf16[384,1536]{1,0:T(8,128)(2,1)}, bf16[384,1536]{1,0:T(8,128)(2,1)S(1)}, u32[]{:S(2)}, u32[]{:S(2)}) collective-permute-start(bf16[384,1536]{1,0:T(8,128)(2,1)} %get-tuple-element.109), channel_id=1, source_target_pairs={{0,1},{1,0},{2,3},{3,2},{4,5},{5,4},{6,7},{7,6},{8,9},{9,8},{10,11... | collective-permute-start | bytes 3538952 | tf_op jit(solution)/shard_map/ppermute | solution.py:243
  606.8 72.5 %collective-permute-start.33 = (bf16[384,1536]{1,0:T(8,128)(2,1)}, bf16[384,1536]{1,0:T(8,128)(2,1)S(1)}, u32[]{:S(2)}, u32[]{:S(2)}) collective-permute-start(bf16[384,1536]{1,0:T(8,128)(2,1)} %get-tuple-element.110), channel_id=1, source_target_pairs={{0,1},{1,0},{2,3},{3,2},{4,5},{5,4},{6,7},{7,6},{8,9},{9,8},{10,11... | collective-permute-start | bytes 3538952 | tf_op jit(solution)/shard_map/ppermute | solution.py:243
  (118 other events, 1554.6 us)
Sparse Core Ops, SparseCore 0:
  47.4 138.5 all-gather.4
  187.5 85.5 all-gather.6
  302.6 69.7 reduce-scatter.7
  374.5 66.6 reduce-scatter.3
  501.1 66.5 reduce-scatter.5
where the time goes:
time: 709 us; the launch traced here: 704 us
  waiting for transfers between devices  220 us (31%)
  matrix products  197 us (28%)
  starting transfers between devices  92.2 us (13%)
  local copies, waits for them, and re-layouts  89.3 us (13%)
  other arithmetic  59.6 us (8%)
  Pallas kernels  29.8 us (4%)
  between operations  15.6 us (2%)
    ppermute x61, waiting for transfers between devices, send(): return lax.ppermute(value, AXES, table[route])  190 us
    ppermute x61, starting transfers between devices, send(): return lax.ppermute(value, AXES, table[route])  89.8 us
    dot_general x5, matrix products, plain_dot(): return jnp.dot(left_side, right_side, preferred_element_type=jnp.float32)  72.3 us
    dot_general x8, matrix products, trans_dot(): lax.dot_general(left_side, right_side, (((1,), (1,)), ((), ())), preferre...  71.4 us
    dot_general x5, matrix products, outer_dot(): lax.dot_general(left_side, right_side, (((0,), (0,)), ((), ())), preferre...  53.8 us
    unnamed x158, local copies, waits for them, and re-layouts  35.3 us
    reduce_scatter x3, waiting for transfers between devices, ffn_scatter(): lax.psum_scatter(parts, 'dp', scatter_dimension=0, axis_index_groups=line...  22.1 us
    pallas_call x1, Pallas kernels, attend_back(): pl.pallas_call(attend_back_body, grid=(heads,), in_specs=[PER_HEAD, fixed...  16.8 us
  transfers between devices with their start and end apart: 69, of which 30 were waited for; matrix products, arithmetic and copies ran while one was open for 45% of the time, Pallas kernels for 4%

commit v1 on v0

--- a/solution.py
+++ b/solution.py
@@ -258,18 +258,15 @@
     def both_halves(mine):
         return jnp.concatenate(in_order(core, mine, send(mine, "t")), axis=0)
 
-    def after(value, *others):
-        return lax.optimization_barrier((value, *others))[0]
-
-    def square_far(mine, near, *others):
+    def square_far(mine, near):
+        far = send(jnp.stack([mine, near]), "second")
         mine_sib = send(mine, "t")
         near_sib = send(near, "t")
-        far = send(after(jnp.stack([mine, near]), *others), "second")
         far_sib = send(far, "t")
         whole = jnp.concatenate(
             [mine, near, far[0], far[1], mine_sib, near_sib, far_sib[0], far_sib[1]], axis=0
         )
-        return whole, far
+        return whole
 
     def scatter_far(mine, theirs):
         came = send(theirs, "t")
@@ -304,10 +301,10 @@
             parts, "dp", scatter_dimension=0, axis_index_groups=line_groups
         ).reshape(2, rows, quarter)
 
-    def ffn_swap(summed, *others):
+    def ffn_swap(summed):
         came = send(pick(summed, 1 - x_index), "x")
         pair = jnp.stack(in_order(x_index, pick(summed, x_index), came))
-        low, high = in_order(y_index, pair, send(after(pair, *others), "y"))
+        low, high = in_order(y_index, pair, send(pair, "y"))
         whole = jnp.concatenate([low[0], high[0], low[1], high[1]], axis=1)
         return whole[:, :ffn_cols].astype(f32)
 
@@ -361,7 +358,8 @@
         return low, fold(view[cut:], 2, y_index, "y")
 
     def scatter_hop2(low, high):
-        return jnp.concatenate([fold(low, 1, y_index, "y"), fold(high, 1, x_index, "x")])
+        low = fold(low, 1, y_index, "y")
+        return jnp.concatenate([low, fold(high, 1, x_index, "x")])
 
     def scatter_line(blocks):
         total = pick(blocks, z_index).astype(f32)
@@ -377,18 +375,18 @@
     qkv_cols = query_cols + 2 * key_cols
     gains = jnp.pad(jnp.stack([attn_gain, ffn_gain], axis=1), ((0, 0), (0, HD - 2)))
 
-    qkv_pieces = line_sends(jnp.concatenate([w_query, w_key, w_value, gains], axis=1))
+    qkv_weights = jnp.concatenate([w_query, w_key, w_value, gains], axis=1)
+    qkv_pieces = line_sends(qkv_weights)
     gate_up_pair = ffn_pair([w_gate, w_up])
-    gate_up_full = ffn_gather(after(gate_up_pair, *qkv_pieces))
-    qkv_near = near_sends(after(line_join(qkv_pieces), gate_up_pair))
+    down_pair = ffn_pair([w_down])
+    gate_up_full = ffn_gather(gate_up_pair)
+    down_full = ffn_gather(down_pair)
+    qkv_near = near_sends(line_join(qkv_pieces))
     qkv_full = far_join(*qkv_near)
-    out_pieces = line_sends(after(w_out, *qkv_near))
-    out_near = near_sends(after(line_join(out_pieces), qkv_full))
+    out_near = near_sends(line_join(line_sends(w_out)))
     out_full = far_join(*out_near)
-    down_pair = ffn_pair([after(w_down, out_full)])
-    down_full = ffn_gather(after(down_pair, gate_up_pair))
     cot_half = my_half(cotangent)
-    cot_near = send(after(cot_half, out_full), "first")
+    cot_near = send(cot_half, "first")
 
     _, position = layout(lengths[0])
     cosine, sine_table = angles(position)
@@ -397,7 +395,6 @@
     start = (jnp.arange(SEQ, dtype=jnp.int32) - position)[:, None]
     stream = inputs.astype(f32)
     inv_one = lax.rsqrt(jnp.mean(stream * stream, axis=-1, keepdims=True) + EPSILON)
-    qkv_full = after(qkv_full, cosine, signed_sine, start, inv_one)
     gain_one = qkv_full[:, qkv_cols].astype(f32)
     gain_two = qkv_full[:, qkv_cols + 1].astype(f32)
     qkv_full = qkv_full[:, :qkv_cols]
@@ -405,9 +402,7 @@
     h_one = (stream * inv_one * gain_one).astype(bf16)
     qkv_bias = jnp.concatenate([b_query, b_key, b_value]).astype(f32)
     qkv_pre = plain_dot(h_one, qkv_full) + qkv_bias
-    q_rot, k_rot, v_low, attended, lse = attend(
-        after(qkv_pre, *out_near), cosine, signed_sine, start
-    )
+    q_rot, k_rot, v_low, attended, lse = attend(qkv_pre, cosine, signed_sine, start)
     branch = trans_dot(attended, out_full)
     resid = (
         my_half(stream)
@@ -416,14 +411,14 @@
     )
     inv_two = lax.rsqrt(jnp.mean(resid * resid, axis=-1, keepdims=True) + EPSILON)
     norm_two = resid * inv_two
-    h_two_half = after((norm_two * gain_two).astype(bf16), cot_near)
-    h_two, h_two_far = square_far(h_two_half, send(h_two_half, "first"))
-    cot_all, _ = square_far(cot_half, cot_near, h_two_far)
+    h_two_half = (norm_two * gain_two).astype(bf16)
+    h_two = square_far(h_two_half, send(h_two_half, "first"))
+    cot_all = square_far(cot_half, cot_near)
 
     gate_full = gate_up_full[:, :quarter]
     up_full = gate_up_full[:, quarter:]
     gate_low = plain_dot(h_two, gate_full).astype(bf16)
-    up_low = plain_dot(after(h_two, gate_low), up_full).astype(bf16)
+    up_low = plain_dot(h_two, up_full).astype(bf16)
     gate_pre = gate_low.astype(f32)
     up_pre = up_low.astype(f32)
     sigmoid_gate = jax.nn.sigmoid(gate_pre)
@@ -431,52 +426,53 @@
     hidden = (swish_gate * up_pre).astype(bf16)
     down_part = outer_dot(cot_all, hidden).astype(bf16)
     down_sum = ffn_scatter(down_part)
-    d_hidden = plain_dot(after(cot_all, down_part), down_full)
-    d_gate = (d_hidden * up_pre * sigmoid_gate * (1.0 + gate_pre * (1.0 - sigmoid_gate))).astype(
-        bf16
-    )
+    late_cot, _ = lax.optimization_barrier((cot_all, down_part))
+    d_hidden = plain_dot(late_cot, down_full)
+    slope = sigmoid_gate * (1.0 + gate_pre * (1.0 - sigmoid_gate))
+    d_gate = (d_hidden * up_pre * slope).astype(bf16)
     d_up = (d_hidden * swish_gate).astype(bf16)
     mid = 4 * half
-    low_hidden = after(hidden, d_gate)
-    ffn_theirs = trans_dot(low_hidden[mid:], down_full).astype(bf16)
-    gate_part = outer_dot(after(h_two, ffn_theirs), d_gate).astype(bf16)
+    ffn_theirs = trans_dot(hidden[mid:], down_full).astype(bf16)
+    gate_part = outer_dot(h_two, d_gate).astype(bf16)
     gate_sum = ffn_scatter(gate_part)
-    ffn_mine = trans_dot(after(low_hidden[:mid], gate_part), down_full).astype(bf16)
+    ffn_mine = trans_dot(hidden[:mid], down_full).astype(bf16)
     ffn_kept, ffn_came = scatter_far(ffn_mine, ffn_theirs)
 
     def entry(gate_side, up_side):
         return (trans_dot(gate_side, gate_full) + trans_dot(up_side, up_full)).astype(bf16)
 
-    theirs = entry(after(d_gate[mid:], ffn_mine), after(d_up[mid:], ffn_mine))
-    mine = entry(after(d_gate[:mid], theirs), after(d_up[:mid], theirs))
+    theirs = entry(d_gate[mid:], d_up[mid:])
+    mine = entry(d_gate[:mid], d_up[:mid])
     kept, came = scatter_far(mine, theirs)
-    up_part = outer_dot(after(h_two, mine), d_up).astype(bf16)
+    up_part = outer_dot(h_two, d_up).astype(bf16)
     up_sum = ffn_scatter(up_part)
-    d_h_two = scatter_near(kept, after(came, up_part))
-    ffn_total = scatter_near(ffn_kept, after(ffn_came, d_h_two))
-    layer_out = both_halves((resid + ffn_total).astype(bf16))
-
+    d_h_two = scatter_near(kept, came)
+    ffn_total = scatter_near(ffn_kept, ffn_came)
     scaled = d_h_two * gain_two
     d_resid = cot_half.astype(f32) + inv_two * (
         scaled - norm_two * jnp.mean(norm_two * scaled, axis=-1, keepdims=True)
     )
     gain_two_part = jnp.sum(d_h_two * norm_two, axis=0)
     d_out_low = both_halves(d_resid.astype(bf16))
-    out_hop = scatter_hop1(outer_dot(d_out_low, attended).astype(bf16))
+    late_resid, _ = lax.optimization_barrier((resid, d_out_low))
+    layer_out = both_halves((late_resid + ffn_total).astype(bf16))
+    out_part = outer_dot(d_out_low, attended).astype(bf16)
+    out_hop = scatter_hop1(out_part)
     down_grad = ffn_swap(down_sum)
     d_attended = plain_dot(d_out_low, out_full).astype(bf16)
     d_qkv = attend_back(q_rot, k_rot, v_low, d_attended, lse, cosine, signed_sine, start)
-    qkv_part = outer_dot(after(h_one, *out_hop), d_qkv).astype(bf16)
+    qkv_part = outer_dot(h_one, d_qkv).astype(bf16)
     qkv_hop = scatter_hop1(qkv_part)
     out_blocks = scatter_hop2(*out_hop)
     qkv_blocks = scatter_hop2(*qkv_hop)
     out_mine = scatter_line(out_blocks)
-    qkv_mine = scatter_line(after(qkv_blocks, out_mine))
+    qkv_mine = scatter_line(qkv_blocks)
     out_grad = scatter_end(out_mine)
     qkv_grad = scatter_end(qkv_mine)
-    gate_grad = ffn_swap(after(gate_sum, d_out_low), *qkv_hop)
+    gate_grad = ffn_swap(gate_sum)
     entry_one = trans_dot(d_qkv, qkv_full)
-    d_h_one = my_half(entry_one) + send(other_half(entry_one).astype(bf16), "t").astype(f32)
+    came = send(other_half(entry_one).astype(bf16), "t")
+    d_h_one = my_half(entry_one) + came.astype(f32)
     half_inv = my_half(inv_one)
     norm_one = my_half(stream) * half_inv
     scaled = d_h_one * gain_one
@@ -484,7 +480,7 @@
         (
             d_resid
             + half_inv * (scaled - norm_one * jnp.mean(norm_one * scaled, axis=-1, keepdims=True))
-        ).astype(bf16)
+        ).astype(bf16),
     )
     gain_one_part = jnp.sum(d_h_one * norm_one, axis=0)
 
@@ -496,7 +492,7 @@
         small = small + lax.ppermute(small, "dp", [(i, i ^ step) for i in range(dp_count)])
         step *= 2
     small = small.reshape(-1)
-    up_grad = ffn_swap(after(up_sum, gate_grad, qkv_mine, small))
+    up_grad = ffn_swap(up_sum)
     gain_sums = small[: 2 * d_model].reshape(2, dp_count, rows)
     gain_mine = lax.dynamic_index_in_dim(gain_sums, dp_index, 1, keepdims=False)
     gain_mine = gain_mine + send(gain_mine, "t")

time: 709 us -> 740 us (1.044)
  starting transfers between devices: 92.2 us -> 114 us
  local copies, waits for them, and re-layouts: 89.3 us -> 98.2 us
    ppermute x61, waiting for transfers between devices: 190 us -> 148 us  [send(): return lax.ppermute(value, AXES, table[route])]
    reduce_scatter x3, waiting for transfers between devices: 22.1 us -> 58.3 us  [ffn_scatter(): lax.psum_scatter(parts, 'dp', scatter_dimension=0, axis_index_groups=line...]
    ppermute x61, starting transfers between devices: 89.8 us -> 113 us  [send(): return lax.ppermute(value, AXES, table[route])]
    slice x3 -> x0, local copies, waits for them, and re-layouts: 10.1 us -> none  [the longest x1 7.76 us: layer(): mine = entry(after(d_gate[:mid], theirs), after(d_up[:mid], theirs))]
    dynamic_update_slice x16, local copies, waits for them, and re-layouts: 9.41 us -> 18.1 us  [far_join(): lax.dynamic_update_slice(whole, piece[:, None, None], (z, px, py, 0, 0))]
    dynamic_update_slice x7, local copies, waits for them, and re-layouts: 2.97 us -> 10.4 us  [line_join(): whole = lax.dynamic_update_slice(whole, piece[None], spot)]
    unnamed x158 -> x123, local copies, waits for them, and re-layouts: 35.3 us -> 36 us
  transfers between devices with their start and end apart: 69 -> 69, of which waited for: 30 -> 23; matrix products, arithmetic and copies ran while one was open for 45% -> 46% of each run, Pallas kernels for 4% -> 4%
where the time goes in v1:
time: 740 us; the launch traced here: 733 us
  waiting for transfers between devices  217 us (29%)
  matrix products  200 us (27%)
  starting transfers between devices  114 us (15%)
  local copies, waits for them, and re-layouts  98.2 us (13%)
  other arithmetic  57.7 us (8%)
  Pallas kernels  29.8 us (4%)
  between operations  15.4 us (2%)
    ppermute x61, waiting for transfers between devices, send(): return lax.ppermute(value, AXES, table[route])  148 us
    ppermute x61, starting transfers between devices, send(): return lax.ppermute(value, AXES, table[route])  113 us
    dot_general x5, matrix products, plain_dot(): return jnp.dot(left_side, right_side, preferred_element_type=jnp.float32)  74.1 us
    dot_general x8, matrix products, trans_dot(): lax.dot_general(left_side, right_side, (((1,), (1,)), ((), ())), preferre...  68.4 us
    reduce_scatter x3, waiting for transfers between devices, ffn_scatter(): lax.psum_scatter(parts, 'dp', scatter_dimension=0, axis_index_groups=line...  58.3 us
    dot_general x5, matrix products, outer_dot(): lax.dot_general(left_side, right_side, (((0,), (0,)), ((), ())), preferre...  57.9 us
    unnamed x123, local copies, waits for them, and re-layouts  36 us
    dynamic_update_slice x16, local copies, waits for them, and re-layouts, far_join(): lax.dynamic_update_slice(whole, piece[:, None, None], (z, px, py, 0, 0))  18.1 us
  transfers between devices with their start and end apart: 69, of which 23 were waited for; matrix products, arithmetic and copies ran while one was open for 46% of the time, Pallas kernels for 4%

profile of v1, /device:TPU:0, one launch (start us, length us, event | category | flops | bytes accessed | tf_op | source)
XLA Modules:
  0.0 733.2 jit_solution(14059220091749022932)
XLA Ops:
  60.5 33.6 %collective-permute-done.10 = bf16[2,96,768]{2,1,0:T(8,128)(2,1)S(1)} collective-permute-done((bf16[2,96,768]{2,1,0:T(8,128)(2,1)S(1)}, bf16[2,96,768]{2,1,0:T(8,128)(2,1)S(1)}, u32[]{:S(2)}, u32[]{:S(2)}) %collective-permute-start.10) | collective-permute-done | bytes 294944 | tf_op jit(solution)/shard_map/ppermute | solution.py:243
  132.8 13.0 %shard_map.254 = (bf16[768,768]{1,0:T(8,128)(2,1)}, bf16[768,128]{1,0:T(8,128)(2,1)}, bf16[768,128]{1,0:T(8,128)(2,1)}, bf16[768,768]{1,0:T(8,128)(2,1)}, f32[768,128]{1,0:T(8,128)}) custom-call(f32[768,1024]{1,0:T(8,128)} %fusion.34.q_pre.k_pre.v_pre, f32[768,1024]{1,0:T(8,128)} %fusion.34.q_pre.k_pre.v_pre, f32[768,1024]{1,0:T(8,128)} %fusion.34.q_pre.k_pre.v_pre, ...), custom_call_target="tpu_custom_call" | custom-call | tf_op jit(solution)/shard_map/pallas_call | solution.py:150
  166.9 26.5 %collective-permute-done.16 = bf16[2,384,1536]{2,1,0:T(8,128)(2,1)} collective-permute-done((bf16[2,384,1536]{2,1,0:T(8,128)(2,1)S(1)}, bf16[2,384,1536]{2,1,0:T(8,128)(2,1)}, u32[]{:S(2)}, u32[]{:S(2)}) %collective-permute-start.16) | collective-permute-done | bytes 2359328 | tf_op jit(solution)/shard_map/ppermute | solution.py:243
  193.4 9.6 %collective-permute-start.19 = (bf16[2,384,1536]{2,1,0:T(8,128)(2,1)}, bf16[2,384,1536]{2,1,0:T(8,128)(2,1)}, u32[]{:S(2)}, u32[]{:S(2)}) collective-permute-start(bf16[2,384,1536]{2,1,0:T(8,128)(2,1)} %collective-permute-done.16), channel_id=1, source_target_pairs={{0,1},{1,0},{2,3},{3,2},{4,5},{5,4},{6,7},{7,6},{8,9},{9,8},{10,11... | collective-permute-start | bytes 7077896 | tf_op jit(solution)/shard_map/ppermute | solution.py:243
  219.4 14.4 %collective-permute-done.21 = bf16[2,384,1536]{2,1,0:T(8,128)(2,1)} collective-permute-done((bf16[2,384,1536]{2,1,0:T(8,128)(2,1)}, bf16[2,384,1536]{2,1,0:T(8,128)(2,1)}, u32[]{:S(2)}, u32[]{:S(2)}) %collective-permute-start.21) | collective-permute-done | bytes 2359328 | tf_op jit(solution)/shard_map/ppermute | solution.py:243
  247.8 18.5 %convolution_convert_fusion.1 = bf16[3072,1152]{1,0:T(8,128)(2,1)} fusion(bf16[3072,1536]{1,0:T(8,128)(2,1)} %fusion.43, bf16[1536,2304]{1,0:T(8,128)(2,1)} %bitcast.441), kind=kOutput, calls=%fused_computation.15 | convolution fusion | flops 10875174912 | bytes 20054016 | tf_op jit(solution)/shard_map/dot_general | solution.py:38
  266.3 21.6 %fusion = (bf16[3072,1152]{1,0:T(8,128)(2,1)}, bf16[3072,1152]{1,0:T(8,128)(2,1)}) fusion(bf16[3072,1152]{1,0:T(8,128)(2,1)} %convolution_convert_fusion.1, bf16[3072,1536]{1,0:T(8,128)(2,1)} %fusion.43, bf16[1536,2304]{1,0:T(8,128)(2,1)} %bitcast.442), kind=kOutput, calls=%fused_computation.5 | convolution fusion | flops 10903486464 | bytes 34209792 | tf_op jit(solution)/shard_map/dot_general | solution.py:38
  287.9 17.3 %convolution_convert_fusion.6 = bf16[1536,1152]{1,0:T(8,128)(2,1)} fusion(bf16[3072,1536]{1,0:T(8,128)(2,1)S(1)} %bitcast.436, bf16[3072,1152]{1,0:T(8,128)(2,1)} %get-tuple-element.124), kind=kOutput, calls=%fused_computation.24 | convolution fusion | flops 10873405440 | bytes 20054016 | tf_op jit(solution)/shard_map/dot_general | solution.py:48
  306.1 26.4 %multiply_convert_fusion = (bf16[3072,1152]{1,0:T(8,128)(2,1)}, bf16[3072,1152]{1,0:T(8,128)(2,1)}) fusion(bf16[3072,1152]{1,0:T(8,128)(2,1)} %convolution_convert_fusion.1, bf16[3072,1152]{1,0:T(8,128)(2,1)} %get-tuple-element.125, bf16[3072,1536]{1,0:T(8,128)(2,1)} %fusion.47, bf16[1536,1152]{1,0:T(8,128)(2,1)} %bitcast.449), kind=kOutput, calls=%fused_computation.13 | convolution fusion | flops 10924720128 | bytes 41287680 | tf_op jit(solution)/shard_map/dot_general | solution.py:38
  332.4 17.9 %convolution_convert_fusion.4 = bf16[1536,1152]{1,0:T(8,128)(2,1)} fusion(bf16[3072,1536]{1,0:T(8,128)(2,1)} %fusion.43, bf16[3072,1152]{1,0:T(8,128)(2,1)} %get-tuple-element.48), kind=kOutput, calls=%fused_computation.22 | convolution fusion | flops 10873405440 | bytes 20054016 | tf_op jit(solution)/shard_map/dot_general | solution.py:48
  350.9 9.9 %fusion.11 = f32[1536,1536]{1,0:T(8,128)S(1)} fusion(bf16[3072,1152]{1,0:T(8,128)(2,1)} %get-tuple-element.49, bf16[1536,2304]{1,0:T(8,128)(2,1)} %bitcast.443), kind=kOutput, calls=%fused_computation.35 | convolution fusion | flops 5435817984 | bytes 16515072 | tf_op jit(solution)/shard_map/dot_general | solution.py:42
  360.8 10.3 %add_convert_fusion = bf16[1536,1536]{1,0:T(8,128)(2,1)} fusion(f32[1536,1536]{1,0:T(8,128)S(1)} %fusion.11, bf16[3072,1152]{1,0:T(8,128)(2,1)S(1)} %bitcast.457, bf16[1536,2304]{1,0:T(8,128)(2,1)} %bitcast.444), kind=kOutput, calls=%fused_computation.18 | convolution fusion | flops 5440536576 | bytes 21233664 | tf_op jit(solution)/shard_map/dot_general | solution.py:42
  371.1 16.1 %convolution_convert_fusion.5 = bf16[1536,1152]{1,0:T(8,128)(2,1)} fusion(bf16[3072,1536]{1,0:T(8,128)(2,1)} %fusion.43, bf16[3072,1152]{1,0:T(8,128)(2,1)S(1)} %bitcast.455), kind=kOutput, calls=%fused_computation.23 | convolution fusion | flops 10873405440 | bytes 20054016 | tf_op jit(solution)/shard_map/dot_general | solution.py:48
  389.2 10.2 %convolution_convert_fusion.2 = bf16[1536,1536]{1,0:T(8,128)(2,1)} fusion(bf16[1536,1152]{1,0:T(8,128)(2,1)S(1)} %bitcast.450, bf16[3072,1152]{1,0:T(8,128)(2,1)} %get-tuple-element.124), kind=kOutput, calls=%fused_computation.20 | convolution fusion | flops 5438177280 | bytes 11796480 | tf_op jit(solution)/shard_map/dot_general | solution.py:42
  399.9 11.6 %fusion.14 = f32[1536,1536]{1,0:T(8,128)} fusion(bf16[3072,1152]{1,0:T(8,128)(2,1)} %get-tuple-element.49, bf16[1536,2304]{1,0:T(8,128)(2,1)} %bitcast.445), kind=kOutput, calls=%fused_computation.38 | convolution fusion | flops 5435817984 | bytes 16515072 | tf_op jit(solution)/shard_map/dot_general | solution.py:42
  411.5 10.6 %convert_add_fusion.1 = f32[1536,1536]{1,0:T(8,128)S(1)} fusion(bf16[1536,1536]{1,0:T(8,128)(2,1)} %collective-permute-done.27, f32[1536,1536]{1,0:T(8,128)} %fusion.14, bf16[3072,1152]{1,0:T(8,128)(2,1)} %get-tuple-element.48, bf16[1536,2304]{1,0:T(8,128)(2,1)S(1)} %bitcast.448), kind=kOutput, calls=%fused_computation.17 | convolution fusion | flops 5447614464 | bytes 30670848 | tf_op jit(solution)/shard_map/dot_general | solution.py:42
  426.7 9.0 %convert_add_fusion = f32[1536,1536]{1,0:T(8,128)S(1)} fusion(bf16[1536,1536]{1,0:T(8,128)(2,1)} %collective-permute-done.31, bf16[1536,1152]{1,0:T(8,128)(2,1)S(1)} %bitcast.451, bf16[3072,1152]{1,0:T(8,128)(2,1)} %get-tuple-element.124), kind=kOutput, calls=%fused_computation.16 | convolution fusion | flops 5445255168 | bytes 21233664 | tf_op jit(solution)/shard_map/dot_general | solution.py:42
  452.9 58.3 %reduce-scatter.4.cloned.1.call-done = bf16[1,384,1152]{2,1,0:T(8,128)(2,1)} async-done(((bf16[4,384,1152]{2,1,0:T(8,128)(2,1)}), bf16[1,384,1152]{2,1,0:T(8,128)(2,1)}) %reduce-scatter.4.cloned.1.call-update) | async-done | bytes 884752 | tf_op jit(solution)/shard_map/reduce_scatter | solution.py:300
  528.2 8.4 %collective-permute-done.29 = bf16[384,1536]{1,0:T(8,128)(2,1)S(1)} collective-permute-done((bf16[384,1536]{1,0:T(8,128)(2,1)S(1)}, bf16[384,1536]{1,0:T(8,128)(2,1)S(1)}, u32[]{:S(2)}, u32[]{:S(2)}) %collective-permute-start.29) | collective-permute-done | bytes 1179680 | tf_op jit(solution)/shard_map/ppermute | solution.py:243
  540.3 8.8 %collective-permute-done.33 = bf16[384,1536]{1,0:T(8,128)(2,1)S(1)} collective-permute-done((bf16[384,1536]{1,0:T(8,128)(2,1)S(1)}, bf16[384,1536]{1,0:T(8,128)(2,1)S(1)}, u32[]{:S(2)}, u32[]{:S(2)}) %collective-permute-start.33) | collective-permute-done | bytes 1179680 | tf_op jit(solution)/shard_map/ppermute | solution.py:243
  549.8 13.4 %collective-permute-start.34 = (bf16[384,1536]{1,0:T(8,128)(2,1)S(1)}, bf16[384,1536]{1,0:T(8,128)(2,1)}, u32[]{:S(2)}, u32[]{:S(2)}) collective-permute-start(bf16[384,1536]{1,0:T(8,128)(2,1)S(1)} %fusion.28), channel_id=1, source_target_pairs={{0,1},{1,0},{2,3},{3,2},{4,5},{5,4},{6,7},{7,6},{8,9},{9,8},{10,11... | collective-permute-start | bytes 3538952 | tf_op jit(solution)/shard_map/ppermute | solution.py:243
  567.9 16.6 %collective-permute-done.59 = bf16[2,192,1152]{2,1,0:T(8,128)(2,1)S(1)} collective-permute-done((bf16[2,192,1152]{2,1,0:T(8,128)(2,1)S(1)}, bf16[2,192,1152]{2,1,0:T(8,128)(2,1)S(1)}, u32[]{:S(2)}, u32[]{:S(2)}) %collective-permute-start.59) | collective-permute-done | bytes 884768 | tf_op jit(solution)/shard_map/ppermute | solution.py:243
  599.2 16.8 %shard_map.255 = bf16[768,1024]{1,0:T(8,128)(2,1)} custom-call(bf16[768,768]{1,0:T(8,128)(2,1)} %get-tuple-element.24.q_rot, bf16[768,128]{1,0:T(8,128)(2,1)} %get-tuple-element.25.k_rot, bf16[768,128]{1,0:T(8,128)(2,1)} %get-tuple-element.26.v_low, bf16[768,768]{1,0:T(8,128)(2,1)} %convolution_convert_fusion.9.d_att, f32[768,128]{1,0:T(8,128)} %get-tuple-element.27.lse, ...), custom_call_target="tpu_custom_call" | custom-call | tf_op jit(solution)/shard_map/pallas_call | solution.py:169
  629.4 22.9 %collective-permute-start.35 = (bf16[384,1536]{1,0:T(8,128)(2,1)S(1)}, bf16[384,1536]{1,0:T(8,128)(2,1)S(1)}, u32[]{:S(2)}, u32[]{:S(2)}) collective-permute-start(bf16[384,1536]{1,0:T(8,128)(2,1)S(1)} %fusion.40), channel_id=1, source_target_pairs={{0,1},{1,0},{2,3},{3,2},{4,5},{5,4},{6,7},{7,6},{8,9},{9,8},{10,11... | collective-permute-start | bytes 3538952 | tf_op jit(solution)/shard_map/ppermute | solution.py:243
  (427 shorter events, 296.1 us)
Async XLA Ops:
  7.2 240.6 %all-gather.5.cloned.1.call-start = ((), (), s32[]{:S(2)}) async-start(), calls=%async_computation.6 | async-start | bytes 8847360 | tf_op jit(solution)/shard_map/all_gather | solution.py:295
  39.8 66.3 %collective-permute-start.25 = (bf16[192,2304]{1,0:T(8,128)(2,1)}, bf16[192,2304]{1,0:T(8,128)(2,1)S(1)}, u32[]{:S(2)}, u32[]{:S(2)}) collective-permute-start(bf16[192,2304]{1,0:T(8,128)(2,1)} %pad_maximum_fusion.18), channel_id=1, source_target_pairs={{0,2},{1,3},{2,0},{3,1},{4,6},{5,7},{6,4},{7,5},{8,10},{9,11},{10,... | collective-permute-start | bytes 2654216 | tf_op jit(solution)/shard_map/ppermute | solution.py:243
  42.8 107.4 %collective-permute-start.15 = (bf16[384,1536]{1,0:T(8,128)(2,1)S(1)}, bf16[384,1536]{1,0:T(8,128)(2,1)}, u32[]{:S(2)}, u32[]{:S(2)}) collective-permute-start(bf16[384,1536]{1,0:T(8,128)(2,1)S(1)} %bitcast.402), channel_id=1, source_target_pairs={{0,2},{1,17},{2,0},{3,19},{4,6},{5,21},{6,4},{7,23},{8,10},{9,25},... | collective-permute-start | bytes 3538952 | tf_op jit(solution)/shard_map/ppermute | solution.py:243
  50.6 43.5 %collective-permute-start.10 = (bf16[2,96,768]{2,1,0:T(8,128)(2,1)S(1)}, bf16[2,96,768]{2,1,0:T(8,128)(2,1)S(1)}, u32[]{:S(2)}, u32[]{:S(2)}) collective-permute-start(bf16[2,96,768]{2,1,0:T(8,128)(2,1)S(1)} %get-tuple-element.111), channel_id=1, source_target_pairs={{0,2},{1,3},{2,0},{3,1},{4,6},{5,7},{6,4},{7,5},{8,10},{9,11},{10,... | collective-permute-start | bytes 884744 | tf_op jit(solution)/shard_map/ppermute | solution.py:243
  56.6 47.0 %collective-permute-start.3 = (bf16[2,96,1152]{2,1,0:T(8,128)(2,1)S(1)}, bf16[2,96,1152]{2,1,0:T(8,128)(2,1)S(1)}, u32[]{:S(2)}, u32[]{:S(2)}) collective-permute-start(bf16[2,96,1152]{2,1,0:T(8,128)(2,1)S(1)} %get-tuple-element.101), channel_id=1, source_target_pairs={{0,2},{1,3},{2,0},{3,1},{4,6},{5,7},{6,4},{7,5},{8,10},{9,11},{10,... | collective-permute-start | bytes 1327112 | tf_op jit(solution)/shard_map/ppermute | solution.py:243
  58.6 50.0 %collective-permute-start.5 = (bf16[2,96,1152]{2,1,0:T(8,128)(2,1)}, bf16[2,96,1152]{2,1,0:T(8,128)(2,1)}, u32[]{:S(2)}, u32[]{:S(2)}) collective-permute-start(bf16[2,96,1152]{2,1,0:T(8,128)(2,1)} %get-tuple-element.100), channel_id=1, source_target_pairs={{0,16},{1,17},{2,18},{3,19},{4,20},{5,21},{6,22},{7,23},{8,24},{9,... | collective-permute-start | bytes 1327112 | tf_op jit(solution)/shard_map/ppermute | solution.py:243
  108.3 197.7 %all-gather.7.cloned.1.call-start = ((), (), s32[]{:S(2)}) async-start(), calls=%async_computation.7 | async-start | bytes 4423680 | tf_op jit(solution)/shard_map/all_gather | solution.py:295
  151.8 41.7 %collective-permute-start.16 = (bf16[2,384,1536]{2,1,0:T(8,128)(2,1)S(1)}, bf16[2,384,1536]{2,1,0:T(8,128)(2,1)}, u32[]{:S(2)}, u32[]{:S(2)}) collective-permute-start(bf16[2,384,1536]{2,1,0:T(8,128)(2,1)S(1)} %pad_maximum_fusion), channel_id=1, source_target_pairs={{0,16},{1,3},{2,18},{3,1},{4,20},{5,7},{6,22},{7,5},{8,24},{9,11},... | collective-permute-start | bytes 7077896 | tf_op jit(solution)/shard_map/ppermute | solution.py:243
  159.2 43.8 %collective-permute-start.20 = (bf16[384,1536]{1,0:T(8,128)(2,1)S(1)}, bf16[384,1536]{1,0:T(8,128)(2,1)S(1)}, u32[]{:S(2)}, u32[]{:S(2)}) collective-permute-start(bf16[384,1536]{1,0:T(8,128)(2,1)S(1)} %get-tuple-element.39), channel_id=1, source_target_pairs={{0,2},{1,17},{2,0},{3,19},{4,6},{5,21},{6,4},{7,23},{8,10},{9,25},... | collective-permute-start | bytes 3538952 | tf_op jit(solution)/shard_map/ppermute | solution.py:243
  159.9 54.9 %collective-permute-start.17 = (bf16[384,1536]{1,0:T(8,128)(2,1)S(1)}, bf16[384,1536]{1,0:T(8,128)(2,1)}, u32[]{:S(2)}, u32[]{:S(2)}) collective-permute-start(bf16[384,1536]{1,0:T(8,128)(2,1)S(1)} %bitcast.403), channel_id=1, source_target_pairs={{0,1},{1,0},{2,3},{3,2},{4,5},{5,4},{6,7},{7,6},{8,9},{9,8},{10,11... | collective-permute-start | bytes 3538952 | tf_op jit(solution)/shard_map/ppermute | solution.py:243
  207.0 240.8 %reduce-scatter.8.cloned.1.call-start = ((), (), s32[]{:S(2)}) async-start(), calls=%async_computation.5 | async-start | bytes 4423680 | tf_op jit(solution)/shard_map/reduce_scatter | solution.py:300
  305.3 145.9 %reduce-scatter.6.cloned.1.call-start = ((), (), s32[]{:S(2)}) async-start(), calls=%async_computation.4 | async-start | bytes 4423680 | tf_op jit(solution)/shard_map/reduce_scatter | solution.py:300
  350.4 160.9 %reduce-scatter.4.cloned.1.call-start = ((), (), s32[]{:S(2)}) async-start(), calls=%async_computation.3 | async-start | bytes 4423680 | tf_op jit(solution)/shard_map/reduce_scatter | solution.py:300
  422.4 91.5 %collective-permute-start.28 = (bf16[2,384,1536]{2,1,0:T(8,128)(2,1)S(1)}, bf16[2,384,1536]{2,1,0:T(8,128)(2,1)}, u32[]{:S(2)}, u32[]{:S(2)}) collective-permute-start(bf16[2,384,1536]{2,1,0:T(8,128)(2,1)S(1)} %bitcast.422), channel_id=1, source_target_pairs={{0,16},{1,3},{2,18},{3,1},{4,20},{5,7},{6,22},{7,5},{8,24},{9,11},... | collective-permute-start | bytes 7077896 | tf_op jit(solution)/shard_map/ppermute | solution.py:243
  441.0 77.6 %collective-permute-start.32 = (bf16[2,384,1536]{2,1,0:T(8,128)(2,1)}, bf16[2,384,1536]{2,1,0:T(8,128)(2,1)}, u32[]{:S(2)}, u32[]{:S(2)}) collective-permute-start(bf16[2,384,1536]{2,1,0:T(8,128)(2,1)} %bitcast.77), channel_id=1, source_target_pairs={{0,16},{1,3},{2,18},{3,1},{4,20},{5,7},{6,22},{7,5},{8,24},{9,11},... | collective-permute-start | bytes 7077896 | tf_op jit(solution)/shard_map/ppermute | solution.py:243
  449.7 73.1 %collective-permute-start.62 = (bf16[192,1152]{1,0:T(8,128)(2,1)}, bf16[192,1152]{1,0:T(8,128)(2,1)}, u32[]{:S(2)}, u32[]{:S(2)}) collective-permute-start(bf16[192,1152]{1,0:T(8,128)(2,1)} %dynamic-slice_bitcast_fusion), channel_id=1, source_target_pairs={{0,2},{1,3},{2,0},{3,1},{4,6},{5,7},{6,4},{7,5},{8,10},{9,11},{10,... | collective-permute-start | bytes 1327112 | tf_op jit(solution)/shard_map/ppermute | solution.py:243
  452.2 73.4 %collective-permute-start.60 = (bf16[192,1152]{1,0:T(8,128)(2,1)S(1)}, bf16[192,1152]{1,0:T(8,128)(2,1)S(1)}, u32[]{:S(2)}, u32[]{:S(2)}) collective-permute-start(bf16[192,1152]{1,0:T(8,128)(2,1)S(1)} %dynamic-slice_bitcast_fusion.1), channel_id=1, source_target_pairs={{0,2},{1,3},{2,0},{3,1},{4,6},{5,7},{6,4},{7,5},{8,10},{9,11},{10,... | collective-permute-start | bytes 1327112 | tf_op jit(solution)/shard_map/ppermute | solution.py:243
  526.6 57.9 %collective-permute-start.59 = (bf16[2,192,1152]{2,1,0:T(8,128)(2,1)S(1)}, bf16[2,192,1152]{2,1,0:T(8,128)(2,1)S(1)}, u32[]{:S(2)}, u32[]{:S(2)}) collective-permute-start(bf16[2,192,1152]{2,1,0:T(8,128)(2,1)S(1)} %pad_maximum_fusion.20), channel_id=1, source_target_pairs={{0,16},{1,17},{2,18},{3,19},{4,20},{5,21},{6,22},{7,23},{8,24},{9,... | collective-permute-start | bytes 2654216 | tf_op jit(solution)/shard_map/ppermute | solution.py:243
  539.6 47.2 %collective-permute-start.30 = (bf16[384,1536]{1,0:T(8,128)(2,1)S(1)}, bf16[384,1536]{1,0:T(8,128)(2,1)S(1)}, u32[]{:S(2)}, u32[]{:S(2)}) collective-permute-start(bf16[384,1536]{1,0:T(8,128)(2,1)S(1)} %get-tuple-element.34), channel_id=1, source_target_pairs={{0,1},{1,0},{2,3},{3,2},{4,5},{5,4},{6,7},{7,6},{8,9},{9,8},{10,11... | collective-permute-start | bytes 3538952 | tf_op jit(solution)/shard_map/ppermute | solution.py:243
  549.8 76.5 %collective-permute-start.34 = (bf16[384,1536]{1,0:T(8,128)(2,1)S(1)}, bf16[384,1536]{1,0:T(8,128)(2,1)}, u32[]{:S(2)}, u32[]{:S(2)}) collective-permute-start(bf16[384,1536]{1,0:T(8,128)(2,1)S(1)} %fusion.28), channel_id=1, source_target_pairs={{0,1},{1,0},{2,3},{3,2},{4,5},{5,4},{6,7},{7,6},{8,9},{9,8},{10,11... | collective-permute-start | bytes 3538952 | tf_op jit(solution)/shard_map/ppermute | solution.py:243
  592.2 60.1 %collective-permute-start.52 = (bf16[2,2,96,768]{3,2,0,1:T(8,128)(2,1)}, bf16[2,2,96,768]{3,2,0,1:T(8,128)(2,1)}, u32[]{:S(2)}, u32[]{:S(2)}) collective-permute-start(bf16[2,2,96,768]{3,2,0,1:T(8,128)(2,1)} %bitcast.395), channel_id=1, source_target_pairs={{0,16},{1,17},{2,18},{3,19},{4,20},{5,21},{6,22},{7,23},{8,24},{9,... | collective-permute-start | bytes 1769480 | tf_op jit(solution)/shard_map/ppermute | solution.py:243
  595.4 59.7 %collective-permute-start.50 = (bf16[2,2,96,768]{3,2,0,1:T(8,128)(2,1)}, bf16[2,2,96,768]{3,2,0,1:T(8,128)(2,1)}, u32[]{:S(2)}, u32[]{:S(2)}) collective-permute-start(bf16[2,2,96,768]{3,2,0,1:T(8,128)(2,1)} %bitcast.396), channel_id=1, source_target_pairs={{0,2},{1,3},{2,0},{3,1},{4,6},{5,7},{6,4},{7,5},{8,10},{9,11},{10,... | collective-permute-start | bytes 1769480 | tf_op jit(solution)/shard_map/ppermute | solution.py:243
  621.8 47.3 %collective-permute-start.42 = (bf16[2,2,96,1024]{3,2,0,1:T(8,128)(2,1)S(1)}, bf16[2,2,96,1024]{3,2,0,1:T(8,128)(2,1)S(1)}, u32[]{:S(2)}, u32[]{:S(2)}) collective-permute-start(bf16[2,2,96,1024]{3,2,0,1:T(8,128)(2,1)S(1)} %bitcast.432), channel_id=1, source_target_pairs={{0,2},{1,3},{2,0},{3,1},{4,6},{5,7},{6,4},{7,5},{8,10},{9,11},{10,... | collective-permute-start | bytes 2359304 | tf_op jit(solution)/shard_map/ppermute | solution.py:243
  629.4 63.9 %collective-permute-start.35 = (bf16[384,1536]{1,0:T(8,128)(2,1)S(1)}, bf16[384,1536]{1,0:T(8,128)(2,1)S(1)}, u32[]{:S(2)}, u32[]{:S(2)}) collective-permute-start(bf16[384,1536]{1,0:T(8,128)(2,1)S(1)} %fusion.40), channel_id=1, source_target_pairs={{0,1},{1,0},{2,3},{3,2},{4,5},{5,4},{6,7},{7,6},{8,9},{9,8},{10,11... | collective-permute-start | bytes 3538952 | tf_op jit(solution)/shard_map/ppermute | solution.py:243
  (101 other events, 1931.1 us)
Sparse Core Ops, SparseCore 0:
  108.5 127.8 all-gather.4
  237.9 68.0 all-gather.6
  308.4 65.0 reduce-scatter.7
  375.7 66.6 reduce-scatter.5
  444.6 66.6 reduce-scatter.3

commit v2 on v1

--- a/solution.py
+++ b/solution.py
@@ -268,15 +268,20 @@
         )
         return whole
 
-    def scatter_far(mine, theirs):
+    quad = 2 * half
+
+    def scatter_far(product, theirs):
         came = send(theirs, "t")
-        total = (mine.astype(f32) + came.astype(f32)).reshape(4, half, d_model)
-        return total[:2], send(total[2:].astype(bf16), "second")
+        far = product(slice(quad, 2 * quad)) + came[quad:].astype(f32)
+        far = far.astype(bf16).reshape(2, half, d_model)
+        came_far = send(far, "second")
+        kept = product(slice(0, quad)) + came[:quad].astype(f32)
+        return kept.reshape(2, half, d_model), came_far
 
     def scatter_near(kept, came):
-        total = kept + came.astype(f32)
-        came = send(total[1].astype(bf16), "first")
-        return total[0] + came.astype(f32)
+        near = (kept[1] + came[1].astype(f32)).astype(bf16)
+        came_near = send(near, "first")
+        return kept[0] + came[0].astype(f32) + came_near.astype(f32)
 
     def ffn_quarter(weight, index):
         parts = [weight[:, i * quarter : (i + 1) * quarter] for i in range(4)]
@@ -435,15 +440,13 @@
     ffn_theirs = trans_dot(hidden[mid:], down_full).astype(bf16)
     gate_part = outer_dot(h_two, d_gate).astype(bf16)
     gate_sum = ffn_scatter(gate_part)
-    ffn_mine = trans_dot(hidden[:mid], down_full).astype(bf16)
-    ffn_kept, ffn_came = scatter_far(ffn_mine, ffn_theirs)
-
-    def entry(gate_side, up_side):
-        return (trans_dot(gate_side, gate_full) + trans_dot(up_side, up_full)).astype(bf16)
-
-    theirs = entry(d_gate[mid:], d_up[mid:])
-    mine = entry(d_gate[:mid], d_up[:mid])
-    kept, came = scatter_far(mine, theirs)
+    ffn_kept, ffn_came = scatter_far(lambda part: trans_dot(hidden[part], down_full), ffn_theirs)
+
+    def entry(part):
+        return trans_dot(d_gate[part], gate_full) + trans_dot(d_up[part], up_full)
+
+    theirs = entry(slice(mid, 2 * mid)).astype(bf16)
+    kept, came = scatter_far(entry, theirs)
     up_part = outer_dot(h_two, d_up).astype(bf16)
     up_sum = ffn_scatter(up_part)
     d_h_two = scatter_near(kept, came)

time: 740 us -> 740 us (level)
  local copies, waits for them, and re-layouts: 98.2 us -> 85.5 us
  matrix products: 200 us -> 208 us
    dot_general x8 -> x11, matrix products: 68.4 us -> 76.4 us  [trans_dot(): lax.dot_general(left_side, right_side, (((1,), (1,)), ((), ())), preferre...]
    reduce_scatter x3, waiting for transfers between devices: 58.3 us -> 65.9 us  [ffn_scatter(): lax.psum_scatter(parts, 'dp', scatter_dimension=0, axis_index_groups=line...]
    unnamed x123 -> x133, local copies, waits for them, and re-layouts: 36 us -> 30.5 us
where the time goes in v2:
time: 740 us; the launch traced here: 733 us
  waiting for transfers between devices  223 us (30%)
  matrix products  208 us (28%)
  starting transfers between devices  115 us (16%)
  local copies, waits for them, and re-layouts  85.5 us (12%)
  other arithmetic  55.8 us (8%)
  Pallas kernels  30 us (4%)
  between operations  15.5 us (2%)
    ppermute x61, waiting for transfers between devices, send(): return lax.ppermute(value, AXES, table[route])  146 us
    ppermute x61, starting transfers between devices, send(): return lax.ppermute(value, AXES, table[route])  114 us
    dot_general x11, matrix products, trans_dot(): lax.dot_general(left_side, right_side, (((1,), (1,)), ((), ())), preferre...  76.4 us
    dot_general x5, matrix products, plain_dot(): return jnp.dot(left_side, right_side, preferred_element_type=jnp.float32)  73.6 us
    reduce_scatter x3, waiting for transfers between devices, ffn_scatter(): lax.psum_scatter(parts, 'dp', scatter_dimension=0, axis_index_groups=line...  65.9 us
    dot_general x5, matrix products, outer_dot(): lax.dot_general(left_side, right_side, (((0,), (0,)), ((), ())), preferre...  58.4 us
    unnamed x133, local copies, waits for them, and re-layouts  30.5 us
    dynamic_update_slice x16, local copies, waits for them, and re-layouts, far_join(): lax.dynamic_update_slice(whole, piece[:, None, None], (z, px, py, 0, 0))  18 us
  transfers between devices with their start and end apart: 69, of which 23 were waited for; matrix products, arithmetic and copies ran while one was open for 46% of the time, Pallas kernels for 4%

profile of v2, /device:TPU:0, one launch (start us, length us, event | category | flops | bytes accessed | tf_op | source)
XLA Modules:
  0.0 733.1 jit_solution(10521537696112465458)
XLA Ops:
  59.5 34.1 %collective-permute-done.10 = bf16[2,96,768]{2,1,0:T(8,128)(2,1)S(1)} collective-permute-done((bf16[2,96,768]{2,1,0:T(8,128)(2,1)S(1)}, bf16[2,96,768]{2,1,0:T(8,128)(2,1)S(1)}, u32[]{:S(2)}, u32[]{:S(2)}) %collective-permute-start.10) | collective-permute-done | bytes 294944 | tf_op jit(solution)/shard_map/ppermute | solution.py:243
  96.0 7.1 collective-permute-done.3
  132.2 13.1 %shard_map.254 = (bf16[768,768]{1,0:T(8,128)(2,1)}, bf16[768,128]{1,0:T(8,128)(2,1)}, bf16[768,128]{1,0:T(8,128)(2,1)}, bf16[768,768]{1,0:T(8,128)(2,1)}, f32[768,128]{1,0:T(8,128)}) custom-call(f32[768,1024]{1,0:T(8,128)} %fusion.54.q_pre.k_pre.v_pre, f32[768,1024]{1,0:T(8,128)} %fusion.54.q_pre.k_pre.v_pre, f32[768,1024]{1,0:T(8,128)} %fusion.54.q_pre.k_pre.v_pre, ...), custom_call_target="tpu_custom_call" | custom-call | tf_op jit(solution)/shard_map/pallas_call | solution.py:150
  167.5 26.5 %collective-permute-done.16 = bf16[2,384,1536]{2,1,0:T(8,128)(2,1)} collective-permute-done((bf16[2,384,1536]{2,1,0:T(8,128)(2,1)S(1)}, bf16[2,384,1536]{2,1,0:T(8,128)(2,1)}, u32[]{:S(2)}, u32[]{:S(2)}) %collective-permute-start.16) | collective-permute-done | bytes 2359328 | tf_op jit(solution)/shard_map/ppermute | solution.py:243
  194.0 8.3 %collective-permute-start.19 = (bf16[2,384,1536]{2,1,0:T(8,128)(2,1)}, bf16[2,384,1536]{2,1,0:T(8,128)(2,1)}, u32[]{:S(2)}, u32[]{:S(2)}) collective-permute-start(bf16[2,384,1536]{2,1,0:T(8,128)(2,1)} %collective-permute-done.16), channel_id=1, source_target_pairs={{0,1},{1,0},{2,3},{3,2},{4,5},{5,4},{6,7},{7,6},{8,9},{9,8},{10,11... | collective-permute-start | bytes 7077896 | tf_op jit(solution)/shard_map/ppermute | solution.py:243
  218.8 14.2 %collective-permute-done.21 = bf16[2,384,1536]{2,1,0:T(8,128)(2,1)} collective-permute-done((bf16[2,384,1536]{2,1,0:T(8,128)(2,1)}, bf16[2,384,1536]{2,1,0:T(8,128)(2,1)}, u32[]{:S(2)}, u32[]{:S(2)}) %collective-permute-start.21) | collective-permute-done | bytes 2359328 | tf_op jit(solution)/shard_map/ppermute | solution.py:243
  247.0 18.4 %convolution_convert_fusion.1 = bf16[3072,1152]{1,0:T(8,128)(2,1)} fusion(bf16[3072,1536]{1,0:T(8,128)(2,1)} %fusion.61, bf16[1536,2304]{1,0:T(8,128)(2,1)} %bitcast.443), kind=kOutput, calls=%fused_computation.15 | convolution fusion | flops 10875174912 | bytes 20054016 | tf_op jit(solution)/shard_map/dot_general | solution.py:38
  265.4 21.6 %fusion = (bf16[3072,1152]{1,0:T(8,128)(2,1)}, bf16[3072,1152]{1,0:T(8,128)(2,1)}) fusion(bf16[3072,1152]{1,0:T(8,128)(2,1)} %convolution_convert_fusion.1, bf16[3072,1536]{1,0:T(8,128)(2,1)} %fusion.61, bf16[1536,2304]{1,0:T(8,128)(2,1)} %bitcast.444), kind=kOutput, calls=%fused_computation.5 | convolution fusion | flops 10903486464 | bytes 34209792 | tf_op jit(solution)/shard_map/dot_general | solution.py:38
  287.1 17.4 %convolution_convert_fusion.5 = bf16[1536,1152]{1,0:T(8,128)(2,1)} fusion(bf16[3072,1536]{1,0:T(8,128)(2,1)S(1)} %bitcast.438, bf16[3072,1152]{1,0:T(8,128)(2,1)} %get-tuple-element.124), kind=kOutput, calls=%fused_computation.20 | convolution fusion | flops 10873405440 | bytes 20054016 | tf_op jit(solution)/shard_map/dot_general | solution.py:48
  305.6 26.2 %multiply_convert_fusion = (bf16[3072,1152]{1,0:T(8,128)(2,1)}, bf16[3072,1152]{1,0:T(8,128)(2,1)}) fusion(bf16[3072,1152]{1,0:T(8,128)(2,1)} %convolution_convert_fusion.1, bf16[3072,1152]{1,0:T(8,128)(2,1)} %get-tuple-element.125, bf16[3072,1536]{1,0:T(8,128)(2,1)} %fusion.65, bf16[1536,1152]{1,0:T(8,128)(2,1)} %bitcast.453), kind=kOutput, calls=%fused_computation.13 | convolution fusion | flops 10924720128 | bytes 41287680 | tf_op jit(solution)/shard_map/dot_general | solution.py:38
  331.8 18.0 %convolution_convert_fusion.3 = bf16[1536,1152]{1,0:T(8,128)(2,1)} fusion(bf16[3072,1536]{1,0:T(8,128)(2,1)} %fusion.61, bf16[3072,1152]{1,0:T(8,128)(2,1)} %get-tuple-element.48), kind=kOutput, calls=%fused_computation.18 | convolution fusion | flops 10873405440 | bytes 20054016 | tf_op jit(solution)/shard_map/dot_general | solution.py:48
  349.9 11.9 %fusion.10 = f32[1536,1536]{1,0:T(8,128)} fusion(bf16[3072,1152]{1,0:T(8,128)(2,1)} %get-tuple-element.49, bf16[1536,2304]{1,0:T(8,128)(2,1)} %bitcast.445), kind=kOutput, calls=%fused_computation.30 | convolution fusion | flops 5435817984 | bytes 16515072 | tf_op jit(solution)/shard_map/dot_general | solution.py:42
  361.8 12.1 %add_convert_fusion = bf16[1536,1536]{1,0:T(8,128)(2,1)} fusion(f32[1536,1536]{1,0:T(8,128)} %fusion.10, bf16[3072,1152]{1,0:T(8,128)(2,1)} %get-tuple-element.48, bf16[1536,2304]{1,0:T(8,128)(2,1)} %bitcast.446), kind=kOutput, calls=%fused_computation.16 | convolution fusion | flops 5440536576 | bytes 21233664 | tf_op jit(solution)/shard_map/dot_general | solution.py:42
  374.0 8.1 %convolution_convert_fusion.2 = bf16[1536,1536]{1,0:T(8,128)(2,1)} fusion(bf16[1536,1152]{1,0:T(8,128)(2,1)S(1)} %bitcast.454, bf16[3072,1152]{1,0:T(8,128)(2,1)S(1)} %bitcast.460), kind=kOutput, calls=%fused_computation.17 | convolution fusion | flops 5438177280 | bytes 11796480 | tf_op jit(solution)/shard_map/dot_general | solution.py:42
  382.6 16.5 %convolution_convert_fusion.4 = bf16[1536,1152]{1,0:T(8,128)(2,1)} fusion(bf16[3072,1536]{1,0:T(8,128)(2,1)} %fusion.61, bf16[3072,1152]{1,0:T(8,128)(2,1)S(1)} %bitcast.464), kind=kOutput, calls=%fused_computation.19 | convolution fusion | flops 10873405440 | bytes 20054016 | tf_op jit(solution)/shard_map/dot_general | solution.py:48
  412.3 6.6 add_convert_fusion.2
  433.0 7.0 convert_add_fusion.1
  445.0 65.8 %reduce-scatter.4.cloned.1.call-done = bf16[1,384,1152]{2,1,0:T(8,128)(2,1)} async-done(((bf16[4,384,1152]{2,1,0:T(8,128)(2,1)}), bf16[1,384,1152]{2,1,0:T(8,128)(2,1)}) %reduce-scatter.4.cloned.1.call-update) | async-done | bytes 884752 | tf_op jit(solution)/shard_map/reduce_scatter | solution.py:305
  525.2 10.9 %collective-permute-done.29 = bf16[384,1536]{1,0:T(8,128)(2,1)S(1)} collective-permute-done((bf16[384,1536]{1,0:T(8,128)(2,1)S(1)}, bf16[384,1536]{1,0:T(8,128)(2,1)S(1)}, u32[]{:S(2)}, u32[]{:S(2)}) %collective-permute-start.29) | collective-permute-done | bytes 1179680 | tf_op jit(solution)/shard_map/ppermute | solution.py:243
  539.5 9.2 %collective-permute-done.33 = bf16[384,1536]{1,0:T(8,128)(2,1)S(1)} collective-permute-done((bf16[384,1536]{1,0:T(8,128)(2,1)S(1)}, bf16[384,1536]{1,0:T(8,128)(2,1)S(1)}, u32[]{:S(2)}, u32[]{:S(2)}) %collective-permute-start.33) | collective-permute-done | bytes 1179680 | tf_op jit(solution)/shard_map/ppermute | solution.py:243
  550.7 12.5 %collective-permute-start.34 = (bf16[384,1536]{1,0:T(8,128)(2,1)S(1)}, bf16[384,1536]{1,0:T(8,128)(2,1)}, u32[]{:S(2)}, u32[]{:S(2)}) collective-permute-start(bf16[384,1536]{1,0:T(8,128)(2,1)S(1)} %fusion.19), channel_id=1, source_target_pairs={{0,1},{1,0},{2,3},{3,2},{4,5},{5,4},{6,7},{7,6},{8,9},{9,8},{10,11... | collective-permute-start | bytes 3538952 | tf_op jit(solution)/shard_map/ppermute | solution.py:243
  567.8 13.3 %collective-permute-done.59 = bf16[2,192,1152]{2,1,0:T(8,128)(2,1)S(1)} collective-permute-done((bf16[2,192,1152]{2,1,0:T(8,128)(2,1)S(1)}, bf16[2,192,1152]{2,1,0:T(8,128)(2,1)S(1)}, u32[]{:S(2)}, u32[]{:S(2)}) %collective-permute-start.59) | collective-permute-done | bytes 884768 | tf_op jit(solution)/shard_map/ppermute | solution.py:243
  595.7 17.0 %shard_map.255 = bf16[768,1024]{1,0:T(8,128)(2,1)} custom-call(bf16[768,768]{1,0:T(8,128)(2,1)} %get-tuple-element.24.q_rot, bf16[768,128]{1,0:T(8,128)(2,1)} %get-tuple-element.25.k_rot, bf16[768,128]{1,0:T(8,128)(2,1)} %get-tuple-element.26.v_low, bf16[768,768]{1,0:T(8,128)(2,1)} %convolution_convert_fusion.8.d_att, f32[768,128]{1,0:T(8,128)} %get-tuple-element.27.lse, ...), custom_call_target="tpu_custom_call" | custom-call | tf_op jit(solution)/shard_map/pallas_call | solution.py:169
  626.6 23.6 %collective-permute-start.35 = (bf16[384,1536]{1,0:T(8,128)(2,1)S(1)}, bf16[384,1536]{1,0:T(8,128)(2,1)S(1)}, u32[]{:S(2)}, u32[]{:S(2)}) collective-permute-start(bf16[384,1536]{1,0:T(8,128)(2,1)S(1)} %fusion.60), channel_id=1, source_target_pairs={{0,1},{1,0},{2,3},{3,2},{4,5},{5,4},{6,7},{7,6},{8,9},{9,8},{10,11... | collective-permute-start | bytes 3538952 | tf_op jit(solution)/shard_map/ppermute | solution.py:243
  (435 shorter events, 298.3 us)
Async XLA Ops:
  7.2 239.8 %all-gather.5.cloned.1.call-start = ((), (), s32[]{:S(2)}) async-start(), calls=%async_computation.6 | async-start | bytes 8847360 | tf_op jit(solution)/shard_map/all_gather | solution.py:300
  39.2 66.3 %collective-permute-start.25 = (bf16[192,2304]{1,0:T(8,128)(2,1)}, bf16[192,2304]{1,0:T(8,128)(2,1)S(1)}, u32[]{:S(2)}, u32[]{:S(2)}) collective-permute-start(bf16[192,2304]{1,0:T(8,128)(2,1)} %pad_maximum_fusion.18), channel_id=1, source_target_pairs={{0,2},{1,3},{2,0},{3,1},{4,6},{5,7},{6,4},{7,5},{8,10},{9,11},{10,... | collective-permute-start | bytes 2654216 | tf_op jit(solution)/shard_map/ppermute | solution.py:243
  42.3 108.5 %collective-permute-start.15 = (bf16[384,1536]{1,0:T(8,128)(2,1)S(1)}, bf16[384,1536]{1,0:T(8,128)(2,1)}, u32[]{:S(2)}, u32[]{:S(2)}) collective-permute-start(bf16[384,1536]{1,0:T(8,128)(2,1)S(1)} %bitcast.403), channel_id=1, source_target_pairs={{0,2},{1,17},{2,0},{3,19},{4,6},{5,21},{6,4},{7,23},{8,10},{9,25},... | collective-permute-start | bytes 3538952 | tf_op jit(solution)/shard_map/ppermute | solution.py:243
  50.0 43.5 %collective-permute-start.10 = (bf16[2,96,768]{2,1,0:T(8,128)(2,1)S(1)}, bf16[2,96,768]{2,1,0:T(8,128)(2,1)S(1)}, u32[]{:S(2)}, u32[]{:S(2)}) collective-permute-start(bf16[2,96,768]{2,1,0:T(8,128)(2,1)S(1)} %get-tuple-element.111), channel_id=1, source_target_pairs={{0,2},{1,3},{2,0},{3,1},{4,6},{5,7},{6,4},{7,5},{8,10},{9,11},{10,... | collective-permute-start | bytes 884744 | tf_op jit(solution)/shard_map/ppermute | solution.py:243
  56.1 47.0 %collective-permute-start.3 = (bf16[2,96,1152]{2,1,0:T(8,128)(2,1)S(1)}, bf16[2,96,1152]{2,1,0:T(8,128)(2,1)S(1)}, u32[]{:S(2)}, u32[]{:S(2)}) collective-permute-start(bf16[2,96,1152]{2,1,0:T(8,128)(2,1)S(1)} %get-tuple-element.101), channel_id=1, source_target_pairs={{0,2},{1,3},{2,0},{3,1},{4,6},{5,7},{6,4},{7,5},{8,10},{9,11},{10,... | collective-permute-start | bytes 1327112 | tf_op jit(solution)/shard_map/ppermute | solution.py:243
  58.0 50.1 %collective-permute-start.5 = (bf16[2,96,1152]{2,1,0:T(8,128)(2,1)}, bf16[2,96,1152]{2,1,0:T(8,128)(2,1)}, u32[]{:S(2)}, u32[]{:S(2)}) collective-permute-start(bf16[2,96,1152]{2,1,0:T(8,128)(2,1)} %get-tuple-element.100), channel_id=1, source_target_pairs={{0,16},{1,17},{2,18},{3,19},{4,20},{5,21},{6,22},{7,23},{8,24},{9,... | collective-permute-start | bytes 1327112 | tf_op jit(solution)/shard_map/ppermute | solution.py:243
  107.9 197.7 %all-gather.7.cloned.1.call-start = ((), (), s32[]{:S(2)}) async-start(), calls=%async_computation.7 | async-start | bytes 4423680 | tf_op jit(solution)/shard_map/all_gather | solution.py:300
  160.7 53.5 %collective-permute-start.17 = (bf16[384,1536]{1,0:T(8,128)(2,1)S(1)}, bf16[384,1536]{1,0:T(8,128)(2,1)}, u32[]{:S(2)}, u32[]{:S(2)}) collective-permute-start(bf16[384,1536]{1,0:T(8,128)(2,1)S(1)} %bitcast.404), channel_id=1, source_target_pairs={{0,1},{1,0},{2,3},{3,2},{4,5},{5,4},{6,7},{7,6},{8,9},{9,8},{10,11... | collective-permute-start | bytes 3538952 | tf_op jit(solution)/shard_map/ppermute | solution.py:243
  206.4 233.6 %reduce-scatter.8.cloned.1.call-start = ((), (), s32[]{:S(2)}) async-start(), calls=%async_computation.5 | async-start | bytes 4423680 | tf_op jit(solution)/shard_map/reduce_scatter | solution.py:305
  304.5 138.8 %reduce-scatter.6.cloned.1.call-start = ((), (), s32[]{:S(2)}) async-start(), calls=%async_computation.4 | async-start | bytes 4423680 | tf_op jit(solution)/shard_map/reduce_scatter | solution.py:305
  349.8 161.0 %reduce-scatter.4.cloned.1.call-start = ((), (), s32[]{:S(2)}) async-start(), calls=%async_computation.3 | async-start | bytes 4423680 | tf_op jit(solution)/shard_map/reduce_scatter | solution.py:305
  418.8 94.6 %collective-permute-start.28 = (bf16[2,384,1536]{2,1,0:T(8,128)(2,1)}, bf16[2,384,1536]{2,1,0:T(8,128)(2,1)S(1)}, u32[]{:S(2)}, u32[]{:S(2)}) collective-permute-start(bf16[2,384,1536]{2,1,0:T(8,128)(2,1)} %bitcast.72), channel_id=1, source_target_pairs={{0,16},{1,3},{2,18},{3,1},{4,20},{5,7},{6,22},{7,5},{8,24},{9,11},... | collective-permute-start | bytes 7077896 | tf_op jit(solution)/shard_map/ppermute | solution.py:243
  426.1 90.2 %collective-permute-start.32 = (bf16[2,384,1536]{2,1,0:T(8,128)(2,1)}, bf16[2,384,1536]{2,1,0:T(8,128)(2,1)}, u32[]{:S(2)}, u32[]{:S(2)}) collective-permute-start(bf16[2,384,1536]{2,1,0:T(8,128)(2,1)} %bitcast.75), channel_id=1, source_target_pairs={{0,16},{1,3},{2,18},{3,1},{4,20},{5,7},{6,22},{7,5},{8,24},{9,11},... | collective-permute-start | bytes 7077896 | tf_op jit(solution)/shard_map/ppermute | solution.py:243
  441.8 77.6 %collective-permute-start.62 = (bf16[192,1152]{1,0:T(8,128)(2,1)}, bf16[192,1152]{1,0:T(8,128)(2,1)}, u32[]{:S(2)}, u32[]{:S(2)}) collective-permute-start(bf16[192,1152]{1,0:T(8,128)(2,1)} %dynamic-slice_bitcast_fusion), channel_id=1, source_target_pairs={{0,2},{1,3},{2,0},{3,1},{4,6},{5,7},{6,4},{7,5},{8,10},{9,11},{10,... | collective-permute-start | bytes 1327112 | tf_op jit(solution)/shard_map/ppermute | solution.py:243
  444.3 77.8 %collective-permute-start.60 = (bf16[192,1152]{1,0:T(8,128)(2,1)S(1)}, bf16[192,1152]{1,0:T(8,128)(2,1)S(1)}, u32[]{:S(2)}, u32[]{:S(2)}) collective-permute-start(bf16[192,1152]{1,0:T(8,128)(2,1)S(1)} %dynamic-slice_bitcast_fusion.1), channel_id=1, source_target_pairs={{0,2},{1,3},{2,0},{3,1},{4,6},{5,7},{6,4},{7,5},{8,10},{9,11},{10,... | collective-permute-start | bytes 1327112 | tf_op jit(solution)/shard_map/ppermute | solution.py:243
  520.6 42.6 %collective-permute-start.63 = (bf16[2,192,1152]{2,1,0:T(8,128)(2,1)S(1)}, bf16[2,192,1152]{2,1,0:T(8,128)(2,1)S(1)}, u32[]{:S(2)}, u32[]{:S(2)}) collective-permute-start(bf16[2,192,1152]{2,1,0:T(8,128)(2,1)S(1)} %pad_maximum_fusion.22), channel_id=1, source_target_pairs={{0,16},{1,17},{2,18},{3,19},{4,20},{5,21},{6,22},{7,23},{8,24},{9,... | collective-permute-start | bytes 2654216 | tf_op jit(solution)/shard_map/ppermute | solution.py:243
  522.4 43.1 %collective-permute-start.61 = (bf16[2,192,1152]{2,1,0:T(8,128)(2,1)S(1)}, bf16[2,192,1152]{2,1,0:T(8,128)(2,1)S(1)}, u32[]{:S(2)}, u32[]{:S(2)}) collective-permute-start(bf16[2,192,1152]{2,1,0:T(8,128)(2,1)S(1)} %pad_maximum_fusion.21), channel_id=1, source_target_pairs={{0,16},{1,17},{2,18},{3,19},{4,20},{5,21},{6,22},{7,23},{8,24},{9,... | collective-permute-start | bytes 2654216 | tf_op jit(solution)/shard_map/ppermute | solution.py:243
  523.6 57.5 %collective-permute-start.59 = (bf16[2,192,1152]{2,1,0:T(8,128)(2,1)S(1)}, bf16[2,192,1152]{2,1,0:T(8,128)(2,1)S(1)}, u32[]{:S(2)}, u32[]{:S(2)}) collective-permute-start(bf16[2,192,1152]{2,1,0:T(8,128)(2,1)S(1)} %pad_maximum_fusion.20), channel_id=1, source_target_pairs={{0,16},{1,17},{2,18},{3,19},{4,20},{5,21},{6,22},{7,23},{8,24},{9,... | collective-permute-start | bytes 2654216 | tf_op jit(solution)/shard_map/ppermute | solution.py:243
  539.5 43.9 %collective-permute-start.30 = (bf16[384,1536]{1,0:T(8,128)(2,1)S(1)}, bf16[384,1536]{1,0:T(8,128)(2,1)S(1)}, u32[]{:S(2)}, u32[]{:S(2)}) collective-permute-start(bf16[384,1536]{1,0:T(8,128)(2,1)S(1)} %get-tuple-element.34), channel_id=1, source_target_pairs={{0,1},{1,0},{2,3},{3,2},{4,5},{5,4},{6,7},{7,6},{8,9},{9,8},{10,11... | collective-permute-start | bytes 3538952 | tf_op jit(solution)/shard_map/ppermute | solution.py:243
  550.7 72.8 %collective-permute-start.34 = (bf16[384,1536]{1,0:T(8,128)(2,1)S(1)}, bf16[384,1536]{1,0:T(8,128)(2,1)}, u32[]{:S(2)}, u32[]{:S(2)}) collective-permute-start(bf16[384,1536]{1,0:T(8,128)(2,1)S(1)} %fusion.19), channel_id=1, source_target_pairs={{0,1},{1,0},{2,3},{3,2},{4,5},{5,4},{6,7},{7,6},{8,9},{9,8},{10,11... | collective-permute-start | bytes 3538952 | tf_op jit(solution)/shard_map/ppermute | solution.py:243
  588.8 61.5 %collective-permute-start.52 = (bf16[2,2,96,768]{3,2,0,1:T(8,128)(2,1)}, bf16[2,2,96,768]{3,2,0,1:T(8,128)(2,1)}, u32[]{:S(2)}, u32[]{:S(2)}) collective-permute-start(bf16[2,2,96,768]{3,2,0,1:T(8,128)(2,1)} %bitcast.398), channel_id=1, source_target_pairs={{0,16},{1,17},{2,18},{3,19},{4,20},{5,21},{6,22},{7,23},{8,24},{9,... | collective-permute-start | bytes 1769480 | tf_op jit(solution)/shard_map/ppermute | solution.py:243
  592.0 61.0 %collective-permute-start.50 = (bf16[2,2,96,768]{3,2,0,1:T(8,128)(2,1)}, bf16[2,2,96,768]{3,2,0,1:T(8,128)(2,1)}, u32[]{:S(2)}, u32[]{:S(2)}) collective-permute-start(bf16[2,2,96,768]{3,2,0,1:T(8,128)(2,1)} %bitcast.399), channel_id=1, source_target_pairs={{0,2},{1,3},{2,0},{3,1},{4,6},{5,7},{6,4},{7,5},{8,10},{9,11},{10,... | collective-permute-start | bytes 1769480 | tf_op jit(solution)/shard_map/ppermute | solution.py:243
  618.6 48.9 %collective-permute-start.42 = (bf16[2,2,96,1024]{3,2,0,1:T(8,128)(2,1)S(1)}, bf16[2,2,96,1024]{3,2,0,1:T(8,128)(2,1)S(1)}, u32[]{:S(2)}, u32[]{:S(2)}) collective-permute-start(bf16[2,2,96,1024]{3,2,0,1:T(8,128)(2,1)S(1)} %bitcast.434), channel_id=1, source_target_pairs={{0,2},{1,3},{2,0},{3,1},{4,6},{5,7},{6,4},{7,5},{8,10},{9,11},{10,... | collective-permute-start | bytes 2359304 | tf_op jit(solution)/shard_map/ppermute | solution.py:243
  626.6 66.7 %collective-permute-start.35 = (bf16[384,1536]{1,0:T(8,128)(2,1)S(1)}, bf16[384,1536]{1,0:T(8,128)(2,1)S(1)}, u32[]{:S(2)}, u32[]{:S(2)}) collective-permute-start(bf16[384,1536]{1,0:T(8,128)(2,1)S(1)} %fusion.60), channel_id=1, source_target_pairs={{0,1},{1,0},{2,3},{3,2},{4,5},{5,4},{6,7},{7,6},{8,9},{9,8},{10,11... | collective-permute-start | bytes 3538952 | tf_op jit(solution)/shard_map/ppermute | solution.py:243
  (105 other events, 2004.8 us)
Sparse Core Ops, SparseCore 0:
  108.0 127.8 all-gather.4
  237.4 68.0 all-gather.6
  307.9 65.0 reduce-scatter.7
  375.2 66.6 reduce-scatter.5
  444.1 66.6 reduce-scatter.3
